TPU v7x, 32 devices: a whole 2x2x4 slice. The times are simulated.
32 devices in a mesh: dp: 4 (over y, x), graph: 8 (over z, core).
Axes of the slice: x: 2, y: 2, z: 4, core: 2. Of those that a mesh axis runs over, the one named last changes fastest.
Arguments:
- nodes: bfloat16 [4, 128, 768], P('dp', 'graph'), may hold values from -6 to 6
- cotangent: bfloat16 [4, 128, 768], P('dp', 'graph'), may hold values from -16 to 16
- sources: int32 [4, 8192], P('dp', 'graph'), may hold values from 0 to 127
- targets: int32 [4, 8192], P('dp', 'graph'), may hold values from 0 to 127, as said below
- edge_weight: float32 [4, 8192], P('dp', 'graph'), may hold values from 0.2 to 1
- w_first: bfloat16 [1536, 768], replicated, may hold values from -0.15625 to 0.15625
- w_second: bfloat16 [768, 768], replicated, may hold values from -0.21875 to 0.21875
- biases: float32 [2, 768], replicated, may hold values from -3 to 3
- master: float32 [1769472], P(('dp', 'graph')), may hold values from -0.2 to 0.2
- moment_first: float32 [1769472], P(('dp', 'graph')), may hold values from -0.6 to 0.6
- moment_second: float32 [1769472], P(('dp', 'graph')), may hold values from 1 to 30
- bias_first: float32 [2, 768], replicated, may hold values from -12 to 12
- bias_second: float32 [2, 768], replicated, may hold values from 1 to 30
Outputs:
- node_out: bfloat16 [4, 128, 768], P('dp', 'graph')
- node_grad: float32 [4, 128, 768], P('dp', 'graph')
- new_master: float32 [1769472], P(('dp', 'graph'))
- new_first: float32 [1769472], P(('dp', 'graph'))
- new_second: float32 [1769472], P(('dp', 'graph'))
- new_biases: float32 [2, 768], replicated
- new_bias_first: float32 [2, 768], replicated
- new_bias_second: float32 [2, 768], replicated
Inputs may be any that keep to these rules, and one draw needn't show every extreme that they name: `targets`: every node is the target of exactly 64 edges of its structure.
All inputs are finite; a program needn't handle non-finite values.
Results may differ from a plain program's by a relative error of at most 0.0031.
Values may be sent and summed in bfloat16 or wider, within the bound.
No kernel may reach another device: no remote copies, remote signals or barrier semaphores. Data moves between devices by JAX's collectives and lax.ppermute only.
A program may use at most 64 MiB of HBM per device.

v0:
```python
import functools
import math

import jax
import jax.numpy as jnp
from jax import lax
from jax.experimental import pallas as pl
from jax.experimental.pallas import tpu as pltpu
from jax.sharding import PartitionSpec as P


STEP = 10

beta_one = 0.9
beta_two = 0.999
epsilon = 1e-08
learn_rate = 0.001

F32 = jnp.float32
BF16 = jnp.bfloat16
LANES = 128
EXACT = 256
DIGIT = 16.0

NN = (((1,), (0,)), ((), ()))
NT = (((1,), (1,)), ((), ()))


def dot(a, b, dims):
    return lax.dot_general(a, b, dims, preferred_element_type=F32)


def split_two(x):
    high = x.astype(BF16)
    low = (x - high.astype(F32)).astype(BF16)
    return high, low


def adam_update(param, first, second, grads):
    new_first = beta_one * first + (1.0 - beta_one) * grads
    new_second = beta_two * second + (1.0 - beta_two) * grads * grads
    ratio = (
        new_first
        / (1.0 - beta_one**STEP)
        / (jnp.sqrt(new_second / (1.0 - beta_two**STEP)) + epsilon)
    )
    return (param - learn_rate * ratio, new_first, new_second)


def pack_kernel(quants, *refs):
    sources, out_ref, held, sems = refs[:5], refs[5], refs[6:11], refs[11]
    copies = [
        pltpu.make_async_copy(source, target, sems.at[i])
        for i, (source, target) in enumerate(zip(sources, held))
    ]
    for copy in copies:
        copy.start()
    for copy in copies:
        copy.wait()
    nodes_ref, cot_ref, src_ref, dst_ref, weight_ref = held
    rows, features = nodes_ref.shape
    width = out_ref.shape[1]
    beside = width - features
    rest = features - beside
    half = width - rest
    out_ref[:rows, :features] = nodes_ref[...]
    out_ref[:rows, features:] = cot_ref[:, :beside]
    out_ref[rows:, :rest] = cot_ref[:, beside:]

    src = src_ref[...].astype(F32)
    dst = dst_ref[...].astype(F32)
    weight = weight_ref[...]
    first = weight.astype(BF16).astype(F32)
    second = (weight - first).astype(BF16).astype(F32)
    if quants == 4:
        values = [src, dst, first, second]
    else:
        src_high = jnp.floor(src * (1.0 / DIGIT))
        dst_high = jnp.floor(dst * (1.0 / DIGIT))
        values = [src_high, src - src_high * DIGIT, dst_high, dst - dst_high * DIGIT]
        values += [first, second, weight - first - second, jnp.zeros_like(first)]
    values = jnp.concatenate(values, 0)
    pieces = rows // quants
    stacked = jnp.concatenate(
        [values[:, i * half : (i + 1) * half] for i in range(pieces)], 0
    )
    out_ref[rows:, rest:] = stacked.astype(BF16)


def weight_kernel(split, place_ref, first_ref, second_ref, bias_ref, first_out, second_out, bias_out,
                  held, second_held, bias_held, turned, sems):
    features, part = second_ref.shape[1], second_out.shape[0]
    wide, tall = held.shape[1], second_held.shape[0]
    column = lax.rem(place_ref[0], split) * part
    begin = pl.multiple_of(jnp.minimum(column // LANES * LANES, features - wide), LANES)
    high = pl.multiple_of(jnp.minimum(column // 16 * 16, features - tall), 16)
    columns = pl.ds(begin, wide)
    copies = [
        pltpu.make_async_copy(first_ref.at[:, columns], held, sems.at[0]),
        pltpu.make_async_copy(second_ref.at[pl.ds(high, tall), :], second_held, sems.at[1]),
        pltpu.make_async_copy(bias_ref.at[:, columns], bias_held, sems.at[2]),
    ]
    for copy in copies:
        copy.start()
    for copy in copies:
        copy.wait()
    mine = pl.ds(pl.multiple_of(column - begin, 8), part)
    for i in range(2):
        turned[...] = held[i * features : (i + 1) * features].astype(F32).T
        first_out[i] = turned[mine, :].astype(BF16)
    turned[:, :LANES] = jnp.broadcast_to(bias_held[:1, :], (LANES, wide)).T
    bias_out[...] = turned[mine, :LANES]
    turned[:tall, :] = second_held[...].astype(F32)
    second_out[...] = turned[pl.ds(pl.multiple_of(column - high, 8), part), :].astype(BF16)


def edge_kernel(scale, count, place_ref, *refs):
    blocks = refs[:count]
    first_ref, second_ref, bias_ref = refs[count : count + 3]
    sums_ref, envelope_ref, nodes_ref, cot_ref = refs[count + 3 : count + 7]
    left, left_back, edges, total = refs[count + 7 :]
    graph = place_ref[0]
    features = nodes_ref.shape[1]
    node_total = nodes_ref.shape[0]
    rows = node_total // count
    part = sums_ref.shape[0] // 3
    width = blocks[0].shape[1]
    beside = width - features
    rest = features - beside
    half = width - rest
    quants = edges.shape[1]
    pieces = rows // quants

    for k in range(count):
        at = pl.ds(pl.multiple_of((graph ^ k) * rows, rows), rows)
        nodes_ref[at, :] = blocks[k][:rows, :features]
        cot_ref[at, :beside] = blocks[k][:rows, features:]
        cot_ref[at, beside:] = blocks[k][rows:, :rest]
        numbers = blocks[k][rows:, rest:].astype(F32)
        for i in range(pieces):
            edges[k, :, i * half : (i + 1) * half] = numbers[i * quants : (i + 1) * quants]

    nodes = nodes_ref[...]
    cot = cot_ref[...]
    src_part = dot(first_ref[0], nodes, NT)
    dst_part = dot(first_ref[1], nodes, NT) + bias_ref[:, :1]
    cot_part = dot(second_ref[...], cot, NT)

    src_high, src_low = split_two(0.5 * src_part)
    dst_high, dst_low = split_two(0.5 * dst_part)
    cot_high, cot_low = split_two((0.5 * scale) * cot_part)
    for i, piece in enumerate([src_high, dst_high, src_low, dst_low]):
        left[:, i * node_total : (i + 1) * node_total] = piece
    left_back[:, :node_total] = cot_high
    left_back[:, node_total:] = cot_low
    total[...] = jnp.zeros_like(total)
    kind = BF16 if quants == 4 else F32
    step = edges.shape[2]
    node_at = lax.broadcasted_iota(jnp.int32, (node_total, step), 0).astype(F32).astype(kind)

    def one_hot(row):
        same = node_at == row.astype(kind)
        return jnp.where(same, jnp.ones((), kind), jnp.zeros((), kind)).astype(BF16)

    def body(k, carry):
        numbers = edges[k]
        if quants == 4:
            src, dst = numbers[0:1], numbers[1:2]
            weight = numbers[2:3] + numbers[3:4]
        else:
            src = numbers[0:1] * DIGIT + numbers[1:2]
            dst = numbers[2:3] * DIGIT + numbers[3:4]
            weight = numbers[4:5] + numbers[5:6] + numbers[6:7]
        src_hot, dst_hot = one_hot(src), one_hot(dst)
        hot = jnp.concatenate([src_hot, dst_hot], 0)
        halved = dot(left[...], jnp.concatenate([hot, hot], 0), NN)
        back = dot(left_back[...], jnp.concatenate([dst_hot, dst_hot], 0), NN) * weight
        tilt = jnp.tanh(halved)
        rise = 1.0 + tilt
        active = (halved * rise) * weight
        d_pre = back * (rise * (1.0 + halved * (1.0 - tilt)))
        high = weight.astype(BF16).astype(F32)
        low = weight - high
        tail = jnp.concatenate([high, low, jnp.zeros((14, step), F32)], 0)
        right = jnp.concatenate(
            [active.astype(BF16), d_pre.astype(BF16), tail.astype(BF16)], 0
        )
        total[...] += dot(right, hot, NT)
        return carry

    lax.fori_loop(0, edges.shape[0], body, 0, unroll=8 if quants == 4 else 1)
    sums_ref[:part] = (scale * total[:part, node_total:]).astype(BF16)
    sums_ref[part : 2 * part] = total[part : 2 * part, :node_total].astype(BF16)
    sums_ref[2 * part :] = total[part : 2 * part, node_total:].astype(BF16)
    envelope = scale * (
        total[2 * part : 2 * part + 1, node_total:]
        + total[2 * part + 1 : 2 * part + 2, node_total:]
    )
    envelope_ref[...] = jnp.broadcast_to(envelope, envelope_ref.shape)


def take_rows(ref, start, rows):
    if rows % 8 == 0:
        return ref[pl.ds(pl.multiple_of(start, 8), rows), :]
    tall = row_window(rows)
    base = start // 8 * 8
    window = ref[pl.ds(pl.multiple_of(base, 8), tall), :]
    return pltpu.roll(window, lax.rem(tall - (start - base), tall), 0)[:rows]


def row_window(rows):
    return -(-rows // 8) * 8 + 8


def grad_kernel(split, count, groups, place_ref, *refs):
    blocks = refs[:split]
    nodes_ref, cot_ref, envelope_ref = refs[split : split + 3]
    outs = refs[split + 3 : split + 3 + groups]
    active_ref, src_ref, dst_ref = refs[split + 3 + groups : split + 6 + groups]
    left, src_sum, dst_sum = refs[split + 6 + groups :]
    graph, group = place_ref[0], place_ref[1]
    features = nodes_ref.shape[1]
    part = blocks[0].shape[0] // 3
    share = 3 * features // (groups * count)

    turned = nodes_ref[...].astype(F32).T
    left[:features] = turned
    left[features : 2 * features] = turned
    slot = lax.rem(graph, split)
    for k in range(split):
        start = pl.multiple_of((slot ^ k) * part, 8)
        block = blocks[k][...].astype(F32)
        left[pl.ds(pl.multiple_of(2 * features + start, 8), part), :] = block[:part]
        src_sum[pl.ds(start, part), :] = block[part : 2 * part]
        dst_sum[pl.ds(start, part), :] = block[2 * part :]

    src_all = src_sum[...].astype(BF16)
    dst_all = dst_sum[...].astype(BF16)
    cot = cot_ref[...]
    active_ref[...] = left[2 * features : 3 * features].astype(BF16)
    src_ref[...] = src_all
    dst_ref[...] = dst_all

    kinds = []
    rows = []
    for k in range(groups):
        start = (count * (group ^ k) + graph) * share
        rows.append(take_rows(left, start, share))
        kinds.append(start + lax.broadcasted_iota(jnp.int32, rows[-1].shape, 0))
    rows = jnp.concatenate(rows, 0)
    kinds = jnp.concatenate(kinds, 0)
    zero = jnp.zeros_like(rows)
    from_src = jnp.where(kinds < features, rows, zero).astype(BF16)
    from_dst = jnp.where((kinds >= features) & (kinds < 2 * features), rows, zero).astype(BF16)
    from_act = jnp.where(kinds >= 2 * features, rows, zero).astype(BF16)
    grads = dot(from_src, src_all, NT) + dot(from_dst, dst_all, NT) + dot(from_act, cot, NN)

    ones = jnp.ones((8, dst_all.shape[1]), BF16)
    bias_pre = dot(ones, dst_all, NT)[:1]
    env_high, env_low = split_two(envelope_ref[...])
    bias_out = (dot(env_high, cot, NN) + dot(env_low, cot, NN))[:1]
    pre_high = bias_pre.astype(BF16).astype(F32)
    out_high = bias_out.astype(BF16).astype(F32)
    tail = outs[0].shape[0] - share
    pad = jnp.zeros((tail - 4, features), F32)
    extra = jnp.concatenate(
        [pre_high, bias_pre - pre_high, out_high, bias_out - out_high, pad], 0
    )
    for k in range(groups):
        full = jnp.concatenate([grads[k * share : (k + 1) * share], extra], 0)
        outs[k][...] = full.astype(outs[k].dtype)


def node_kernel(place_ref, active_ref, src_ref, dst_ref, envelope_ref, first_ref, second_ref,
                bias_ref, nodes_ref, cot_ref, out_ref, grad_ref, wide):
    rows, features = nodes_ref.shape
    node_total = active_ref.shape[1]
    at = pl.ds(pl.multiple_of(place_ref[0] * rows, rows), rows)

    def own(ref):
        wide[...] = ref[...].astype(F32).T
        return wide[at, :].astype(BF16)

    active = own(active_ref)
    src = own(src_ref)
    dst = own(dst_ref)
    env = envelope_ref[...]
    column = jnp.broadcast_to(env[:1], (node_total, node_total)).T
    wide[:, :node_total] = column
    env_own = wide[at, :1]
    summed = dot(active, second_ref[...], NN) + env_own * bias_ref[1:2, :]
    out_ref[...] = (nodes_ref[...].astype(F32) + summed).astype(BF16)
    back = dot(src, first_ref[:features], NT) + dot(dst, first_ref[features:], NT)
    grad_ref[...] = cot_ref[...].astype(F32) + back


def adam_kernel(groups, *refs):
    parts = refs[:groups]
    master_ref, first_ref, second_ref, bias_ref, bias_first_ref, bias_second_ref = refs[
        groups : groups + 6
    ]
    outs = refs[groups + 6 : groups + 12]
    flat = refs[groups + 12]
    features = parts[0].shape[1]
    total = parts[0][...]
    for ref in parts[1:]:
        total = total + ref[...].astype(F32)
    total = total * (1.0 / groups)
    across = features // LANES
    share = flat.shape[0] // across
    for q in range(across):
        flat[pl.ds(q, share, stride=across), :] = total[:share, q * LANES : (q + 1) * LANES]
    results = adam_update(master_ref[...], first_ref[...], second_ref[...], flat[...])
    for ref, value in zip(outs[:3], results):
        ref[...] = value
    pairs = total[share : share + 4]
    bias_grads = jnp.concatenate([pairs[0:1] + pairs[1:2], pairs[2:3] + pairs[3:4]], 0)
    results = adam_update(bias_ref[...], bias_first_ref[...], bias_second_ref[...], bias_grads)
    for ref, value in zip(outs[3:], results):
        ref[...] = value


def swap(value, axis, count, distance):
    return lax.ppermute(value, axis, [(i, i ^ distance) for i in range(count)])


def gather_blocks(value, axis, count, reach):
    blocks = {0: value}
    for k in range(reach - 2, 0, -2):
        blocks[k] = swap(value, axis, count, k)
    for k in range(0, reach, 2):
        blocks[k + 1] = swap(blocks[k], axis, count, 1)
    return [blocks[k] for k in range(reach)]


def smem():
    return pl.BlockSpec(memory_space=pltpu.SMEM)


def call(body, ins, outs, scratch=(), place=None, flops=0, room=24 << 20,
         far=()):
    far = set(far)
    arrays = [
        pltpu.with_memory_space_constraint(a, pltpu.HBM) if i in far else a
        for i, a in enumerate(ins)
    ]
    specs = [
        pl.BlockSpec(memory_space=pltpu.HBM if i in far else pltpu.VMEM)
        for i in range(len(arrays))
    ]
    if place is not None:
        arrays = [place] + arrays
        specs = [smem()] + specs
    moved = sum(a.size * a.dtype.itemsize for a in list(ins) + list(outs))
    return pl.pallas_call(
        body,
        out_shape=tuple(outs),
        in_specs=specs,
        out_specs=tuple([pl.BlockSpec(memory_space=pltpu.VMEM)] * len(outs)),
        scratch_shapes=list(scratch),
        compiler_params=pltpu.CompilerParams(vmem_limit_bytes=room),
        cost_estimate=pl.CostEstimate(flops=flops, bytes_accessed=moved, transcendentals=0),
    )(*arrays)


def shards(
    nodes,
    cotangent,
    sources,
    targets,
    edge_weight,
    w_first,
    w_second,
    biases,
    master,
    moment_first,
    moment_second,
    bias_first,
    bias_second,
):
    features = nodes.shape[2]
    rows = nodes.shape[1]
    edge_count = sources.shape[1]
    scale = 1.0 / math.sqrt(edge_count / rows)
    count = lax.axis_size("graph")
    groups = lax.axis_size("dp")
    node_total = rows * count
    split = min(count, 2)
    part = features // split
    share = master.shape[0] // features
    struct = jax.ShapeDtypeStruct
    graph = lax.axis_index("graph")
    group = lax.axis_index("dp")

    over = max(i * part % LANES for i in range(split))
    wide = min(features, -(-(part + over) // LANES) * LANES)
    tall = min(features, part if part % 16 == 0 else -(-part // 16) * 16 + 16)
    place = jnp.stack([graph, group]).astype(jnp.int32)

    quants = 4 if node_total <= EXACT else 8
    width = features + quants * edge_count // (2 * rows)
    sources_in = [nodes[0], cotangent[0], sources, targets, edge_weight]
    (packed,) = call(
        functools.partial(pack_kernel, quants),
        sources_in,
        [struct((2 * rows, width), BF16)],
        [pltpu.VMEM(a.shape, a.dtype) for a in sources_in]
        + [pltpu.SemaphoreType.DMA((len(sources_in),))],
        far=range(len(sources_in)),
    )
    blocks = gather_blocks(packed, "graph", count, count)
    weights = call(
        functools.partial(weight_kernel, split),
        [w_first, w_second, biases],
        [
            struct((2, part, features), BF16),
            struct((part, features), BF16),
            struct((part, LANES), F32),
        ],
        [
            pltpu.VMEM((2 * features, wide), BF16),
            pltpu.VMEM((tall, features), BF16),
            pltpu.VMEM((2, wide), F32),
            pltpu.VMEM((wide, features), F32),
            pltpu.SemaphoreType.DMA((3,)),
        ],
        place=place,
        far=range(3),
    )
    sums, envelope, all_nodes, all_cot = call(
        functools.partial(edge_kernel, scale, count),
        blocks + list(weights),
        [
            struct((3 * part, node_total), BF16),
            struct((8, node_total), F32),
            struct((node_total, features), BF16),
            struct((node_total, features), BF16),
        ],
        [
            pltpu.VMEM((part, 4 * node_total), BF16),
            pltpu.VMEM((part, 2 * node_total), BF16),
            pltpu.VMEM((count, quants, edge_count), F32),
            pltpu.VMEM((2 * part + 16, 2 * node_total), F32),
        ],
        place=place,
        flops=8 * part * 2 * node_total * edge_count * count,
    )
    blocks = gather_blocks(sums, "graph", count, split)
    tall = -(-(share + 4) // 16) * 16
    results = call(
        functools.partial(grad_kernel, split, count, groups),
        blocks + [all_nodes, all_cot, envelope],
        [struct((tall, features), F32)]
        + [struct((tall, features), BF16)] * (groups - 1)
        + [struct((features, node_total), BF16)] * 3,
        [
            pltpu.VMEM((3 * features + 16, node_total), F32),
            pltpu.VMEM((features, node_total), F32),
            pltpu.VMEM((features, node_total), F32),
        ],
        place=place,
        flops=2 * groups * share * 3 * node_total * features,
    )
    grads = results[:groups]
    active, src_sum, dst_sum = results[groups:]
    received = [grads[0]]
    for k in range(1, groups):
        received.append(swap(grads[k], "dp", groups, k))
    node_out, node_grad = call(
        node_kernel,
        [active, src_sum, dst_sum, envelope, w_first, w_second, biases, nodes[0], cotangent[0]],
        [struct((rows, features), BF16), struct((rows, features), F32)],
        [pltpu.VMEM((node_total, features), F32)],
        place=place,
        flops=6 * node_total * features * features,
    )
    lanes = (share * (features // LANES), LANES)
    updated = call(
        functools.partial(adam_kernel, groups),
        received
        + [master.reshape(lanes), moment_first.reshape(lanes), moment_second.reshape(lanes)]
        + [biases, bias_first, bias_second],
        [struct(lanes, F32)] * 3 + [struct(biases.shape, F32)] * 3,
        [pltpu.VMEM(lanes, F32)],
    )
    return (
        node_out[None],
        node_grad[None],
        updated[0].reshape(master.shape),
        updated[1].reshape(master.shape),
        updated[2].reshape(master.shape),
        updated[3],
        updated[4],
        updated[5],
    )


def solution(mesh):
    placed = (
        P("dp", "graph", None),
        P("dp", "graph", None),
        P("dp", "graph"),
        P("dp", "graph"),
        P("dp", "graph"),
        P(),
        P(),
        P(),
        P(("dp", "graph")),
        P(("dp", "graph")),
        P(("dp", "graph")),
        P(),
        P(),
    )
    return jax.shard_map(
        shards,
        mesh=mesh,
        in_specs=placed,
        out_specs=(
            P("dp", "graph", None),
            P("dp", "graph", None),
            P(("dp", "graph")),
            P(("dp", "graph")),
            P(("dp", "graph")),
            P(),
            P(),
            P(),
        ),
        check_vma=False,
    )
```

profile of v0, /device:TPU:0, one launch (start us, length us, event | category | flops | bytes accessed | tf_op | source)
XLA Modules:
  0.0 38.9 jit_solution(16870002021363557890)
XLA Ops:
  0.6 0.8 %shard_map.188.refs_0_ = bf16[32,896]{1,0:T(8,128)(2,1)S(1)} custom-call(bf16[16,768]{1,0:T(8,128)(2,1)} %bitcast.15, bf16[16,768]{1,0:T(8,128)(2,1)} %bitcast.17, s32[1,1024]{1,0:T(1,128)} %refs_2_.1, s32[1,1024]{1,0:T(1,128)} %refs_3_.1, f32[1,1024]{1,0:T(1,128)} %refs_4_.1), custom_call_target="tpu_custom_call" | custom-call | bytes 118784 | tf_op jit(solution)/shard_map/pallas_call | solution.py:355
  1.5 5.1 %collective-permute-start.5 = (bf16[32,896]{1,0:T(8,128)(2,1)S(1)}, bf16[32,896]{1,0:T(8,128)(2,1)S(1)}, u32[]{:S(2)}, u32[]{:S(2)}) collective-permute-start(bf16[32,896]{1,0:T(8,128)(2,1)S(1)} %shard_map.188.refs_0_), channel_id=1, source_target_pairs={{0,6},{1,7},{2,4},{3,5},{4,2},{5,3},{6,0},{7,1},{8,14},{9,15},{10,... | collective-permute-start | bytes 172040 | tf_op jit(solution)/shard_map/ppermute | solution.py:324
  6.6 0.0 collective-permute-start.3
  6.6 0.6 %collective-permute-start.1 = (bf16[32,896]{1,0:T(8,128)(2,1)S(1)}, bf16[32,896]{1,0:T(8,128)(2,1)S(1)}, u32[]{:S(2)}, u32[]{:S(2)}) collective-permute-start(bf16[32,896]{1,0:T(8,128)(2,1)S(1)} %shard_map.188.refs_0_), channel_id=1, source_target_pairs={{0,2},{1,3},{2,0},{3,1},{4,6},{5,7},{6,4},{7,5},{8,10},{9,11},{10,... | collective-permute-start | bytes 172040 | tf_op jit(solution)/shard_map/ppermute | solution.py:324
  7.3 0.0 collective-permute-start
  7.3 1.7 %collective-permute-done.5.refs_6_ = bf16[32,896]{1,0:T(8,128)(2,1)S(1)} collective-permute-done((bf16[32,896]{1,0:T(8,128)(2,1)S(1)}, bf16[32,896]{1,0:T(8,128)(2,1)S(1)}, u32[]{:S(2)}, u32[]{:S(2)}) %collective-permute-start.5) | collective-permute-done | bytes 57376 | tf_op jit(solution)/shard_map/ppermute | solution.py:324
  8.9 0.0 collective-permute-start.6
  8.9 2.8 %collective-permute-done.3.refs_4_ = bf16[32,896]{1,0:T(8,128)(2,1)S(1)} collective-permute-done((bf16[32,896]{1,0:T(8,128)(2,1)S(1)}, bf16[32,896]{1,0:T(8,128)(2,1)S(1)}, u32[]{:S(2)}, u32[]{:S(2)}) %collective-permute-start.3) | collective-permute-done | bytes 57376 | tf_op jit(solution)/shard_map/ppermute | solution.py:324
  11.7 0.0 collective-permute-start.4
  11.7 0.0 collective-permute-done.1.refs_2_
  11.7 0.5 %collective-permute-start.2 = (bf16[32,896]{1,0:T(8,128)(2,1)S(1)}, bf16[32,896]{1,0:T(8,128)(2,1)S(1)}, u32[]{:S(2)}, u32[]{:S(2)}) collective-permute-start(bf16[32,896]{1,0:T(8,128)(2,1)S(1)} %collective-permute-done.1.refs_2_), channel_id=1, source_target_pairs={{0,1},{1,0},{2,3},{3,2},{4,5},{5,4},{6,7},{7,6},{8,9},{9,8},{10,11... | collective-permute-start | bytes 172040 | tf_op jit(solution)/shard_map/ppermute | solution.py:324
  12.2 0.1 pad_add_fusion.place_ref
  12.3 2.7 %shard_map.189 = (bf16[2,384,768]{2,1,0:T(8,128)(2,1)S(1)}, bf16[384,768]{1,0:T(8,128)(2,1)S(1)}, f32[384,128]{1,0:T(8,128)S(1)}) custom-call(s32[2]{0:T(128)S(1)} %pad_add_fusion.place_ref, bf16[1536,768]{1,0:T(8,128)(2,1)} %first_ref.3, bf16[768,768]{1,0:T(8,128)(2,1)} %second_ref.3, f32[2,768]{1,0:T(2,128)} %refs_7_.1), custom_call_target="tpu_custom_call" | custom-call | bytes 5511168 | tf_op jit(solution)/shard_map/pallas_call | solution.py:355
  15.0 0.0 collective-permute-done.refs_1_
  15.0 0.0 collective-permute-done.6.refs_7_
  15.0 0.0 collective-permute-done.4.refs_5_
  15.0 0.0 collective-permute-done.2.refs_3_
  15.0 0.0 copy-start
  15.0 0.0 copy-start.1
  15.1 0.0 copy-start.5
  15.1 0.0 copy-start.6
  15.1 0.0 copy-start.7
  15.1 10.5 %shard_map.190 = (bf16[1152,128]{1,0:T(8,128)(2,1)S(1)}, f32[8,128]{1,0:T(8,128)S(1)}, bf16[128,768]{1,0:T(8,128)(2,1)S(1)}, bf16[128,768]{1,0:T(8,128)(2,1)S(1)}) custom-call(s32[2]{0:T(128)S(1)} %pad_add_fusion.place_ref, bf16[32,896]{1,0:T(8,128)(2,1)S(1)} %shard_map.188.refs_0_, bf16[32,896]{1,0:T(8,128)(2,1)S(1)} %collective-permute-done.refs_1_, ...), custom_call_target="tpu_custom_call" | custom-call | flops 6442450944 | bytes 3117056 | tf_op jit(solution)/shard_map/pallas_call | solution.py:355
  25.6 0.1 collective-permute-start.7
  25.6 1.6 %collective-permute-done.7.refs_1_ = bf16[1152,128]{1,0:T(8,128)(2,1)S(1)} collective-permute-done((bf16[1152,128]{1,0:T(8,128)(2,1)S(1)}, bf16[1152,128]{1,0:T(8,128)(2,1)S(1)}, u32[]{:S(2)}, u32[]{:S(2)}) %collective-permute-start.7) | collective-permute-done | bytes 294944 | tf_op jit(solution)/shard_map/ppermute | solution.py:324
  27.2 1.3 %shard_map.191 = (f32[80,768]{1,0:T(8,128)S(1)}, bf16[80,768]{1,0:T(8,128)(2,1)S(1)}, bf16[80,768]{1,0:T(8,128)(2,1)S(1)}, bf16[80,768]{1,0:T(8,128)(2,1)S(1)}, ...) custom-call(s32[2]{0:T(128)S(1)} %pad_add_fusion.place_ref, ...), custom_call_target="tpu_custom_call" | custom-call | flops 169869312 | bytes 2191360 | tf_op jit(solution)/shard_map/pallas_call | solution.py:355
  28.6 1.6 %collective-permute-start.8 = (bf16[80,768]{1,0:T(8,128)(2,1)S(1)}, bf16[80,768]{1,0:T(8,128)(2,1)S(1)}, u32[]{:S(2)}, u32[]{:S(2)}) collective-permute-start(bf16[80,768]{1,0:T(8,128)(2,1)S(1)} %get-tuple-element.43), channel_id=1, source_target_pairs={{0,8},{8,0},{16,24},{24,16},{1,9},{9,1},{17,25},{25,17},{2,10},{10... | collective-permute-start | bytes 368648 | tf_op jit(solution)/shard_map/ppermute | solution.py:324
  30.1 1.5 %collective-permute-start.9 = (bf16[80,768]{1,0:T(8,128)(2,1)S(1)}, bf16[80,768]{1,0:T(8,128)(2,1)S(1)}, u32[]{:S(2)}, u32[]{:S(2)}) collective-permute-start(bf16[80,768]{1,0:T(8,128)(2,1)S(1)} %get-tuple-element.44), channel_id=1, source_target_pairs={{0,16},{8,24},{16,0},{24,8},{1,17},{9,25},{17,1},{25,9},{2,18},{10... | collective-permute-start | bytes 368648 | tf_op jit(solution)/shard_map/ppermute | solution.py:324
  31.6 0.5 %collective-permute-start.10 = (bf16[80,768]{1,0:T(8,128)(2,1)S(1)}, bf16[80,768]{1,0:T(8,128)(2,1)S(1)}, u32[]{:S(2)}, u32[]{:S(2)}) collective-permute-start(bf16[80,768]{1,0:T(8,128)(2,1)S(1)} %get-tuple-element.45), channel_id=1, source_target_pairs={{0,24},{8,16},{16,8},{24,0},{1,25},{9,17},{17,9},{25,1},{2,26},{10... | collective-permute-start | bytes 368648 | tf_op jit(solution)/shard_map/ppermute | solution.py:324
  32.1 0.0 copy-done
  32.1 0.0 copy-done.1
  32.1 0.0 copy-done.5
  32.1 0.0 copy-done.6
  32.1 0.0 copy-done.7
  32.1 0.0 copy-start.2
  32.1 0.0 copy-start.3
  32.2 0.0 copy-start.4
  32.2 0.0 copy-start.8
  32.2 0.0 copy-start.9
  32.2 2.2 %shard_map.192 = (bf16[16,768]{1,0:T(8,128)(2,1)}, f32[16,768]{1,0:T(8,128)}) custom-call(s32[2]{0:T(128)S(1)} %pad_add_fusion.place_ref, bf16[768,128]{1,0:T(8,128)(2,1)S(1)} %get-tuple-element.37.active_ref, bf16[768,128]{1,0:T(8,128)(2,1)S(1)} %get-tuple-element.38.src_ref, bf16[768,128]{1,0:T(8,128)(2,1)S(1)} %get-tuple-element.39.dst_ref, ...), custom_call_target="tpu_custom_call" | custom-call | flops 452984832 | bytes 4261888 | tf_op jit(solution)/shard_map/pallas_call | solution.py:355
  34.4 0.0 collective-permute-done.8.refs_1_
  34.4 3.5 %collective-permute-done.9.refs_2_ = bf16[80,768]{1,0:T(8,128)(2,1)S(1)} collective-permute-done((bf16[80,768]{1,0:T(8,128)(2,1)S(1)}, bf16[80,768]{1,0:T(8,128)(2,1)S(1)}, u32[]{:S(2)}, u32[]{:S(2)}) %collective-permute-start.9) | collective-permute-done | bytes 122912 | tf_op jit(solution)/shard_map/ppermute | solution.py:324
  37.8 0.0 collective-permute-done.10.refs_3_
  37.8 0.0 copy-done.2
  37.8 0.0 copy-done.3
  37.8 0.0 copy-done.4
  37.9 0.0 copy-done.8
  37.9 1.1 %shard_map.193 = (f32[432,128]{1,0:T(8,128)}, f32[432,128]{1,0:T(8,128)}, f32[432,128]{1,0:T(8,128)}, f32[2,768]{1,0:T(2,128)}, f32[2,768]{1,0:T(2,128)}, /*index=5*/f32[2,768]{1,0:T(2,128)}) custom-call(f32[80,768]{1,0:T(8,128)S(1)} %get-tuple-element.42.refs_0_, bf16[80,768]{1,0:T(8,128)(2,1)S(1)} %collective-permute-done.8.refs_1_, ...), custom_call_target="tpu_custom_call" | custom-call | bytes 1978368 | tf_op jit(solution)/shard_map/pallas_call | solution.py:355
  (1 shorter events, 0.0 us)
Async XLA Ops:
  1.5 7.5 %collective-permute-start.5 = (bf16[32,896]{1,0:T(8,128)(2,1)S(1)}, bf16[32,896]{1,0:T(8,128)(2,1)S(1)}, u32[]{:S(2)}, u32[]{:S(2)}) collective-permute-start(bf16[32,896]{1,0:T(8,128)(2,1)S(1)} %shard_map.188.refs_0_), channel_id=1, source_target_pairs={{0,6},{1,7},{2,4},{3,5},{4,2},{5,3},{6,0},{7,1},{8,14},{9,15},{10,... | collective-permute-start | bytes 172040 | tf_op jit(solution)/shard_map/ppermute | solution.py:324
  6.6 5.1 %collective-permute-start.3 = (bf16[32,896]{1,0:T(8,128)(2,1)S(1)}, bf16[32,896]{1,0:T(8,128)(2,1)S(1)}, u32[]{:S(2)}, u32[]{:S(2)}) collective-permute-start(bf16[32,896]{1,0:T(8,128)(2,1)S(1)} %shard_map.188.refs_0_), channel_id=1, source_target_pairs={{0,4},{1,5},{2,6},{3,7},{4,0},{5,1},{6,2},{7,3},{8,12},{9,13},{10,... | collective-permute-start | bytes 172040 | tf_op jit(solution)/shard_map/ppermute | solution.py:324
  6.6 5.1 %collective-permute-start.1 = (bf16[32,896]{1,0:T(8,128)(2,1)S(1)}, bf16[32,896]{1,0:T(8,128)(2,1)S(1)}, u32[]{:S(2)}, u32[]{:S(2)}) collective-permute-start(bf16[32,896]{1,0:T(8,128)(2,1)S(1)} %shard_map.188.refs_0_), channel_id=1, source_target_pairs={{0,2},{1,3},{2,0},{3,1},{4,6},{5,7},{6,4},{7,5},{8,10},{9,11},{10,... | collective-permute-start | bytes 172040 | tf_op jit(solution)/shard_map/ppermute | solution.py:324
  7.3 7.7 %collective-permute-start = (bf16[32,896]{1,0:T(8,128)(2,1)S(1)}, bf16[32,896]{1,0:T(8,128)(2,1)S(1)}, u32[]{:S(2)}, u32[]{:S(2)}) collective-permute-start(bf16[32,896]{1,0:T(8,128)(2,1)S(1)} %shard_map.188.refs_0_), channel_id=1, source_target_pairs={{0,1},{1,0},{2,3},{3,2},{4,5},{5,4},{6,7},{7,6},{8,9},{9,8},{10,11... | collective-permute-start | bytes 172040 | tf_op jit(solution)/shard_map/ppermute | solution.py:324
  8.9 6.1 %collective-permute-start.6 = (bf16[32,896]{1,0:T(8,128)(2,1)S(1)}, bf16[32,896]{1,0:T(8,128)(2,1)S(1)}, u32[]{:S(2)}, u32[]{:S(2)}) collective-permute-start(bf16[32,896]{1,0:T(8,128)(2,1)S(1)} %collective-permute-done.5.refs_6_), channel_id=1, source_target_pairs={{0,1},{1,0},{2,3},{3,2},{4,5},{5,4},{6,7},{7,6},{8,9},{9,8},{10,11... | collective-permute-start | bytes 172040 | tf_op jit(solution)/shard_map/ppermute | solution.py:324
  11.7 3.3 %collective-permute-start.4 = (bf16[32,896]{1,0:T(8,128)(2,1)S(1)}, bf16[32,896]{1,0:T(8,128)(2,1)S(1)}, u32[]{:S(2)}, u32[]{:S(2)}) collective-permute-start(bf16[32,896]{1,0:T(8,128)(2,1)S(1)} %collective-permute-done.3.refs_4_), channel_id=1, source_target_pairs={{0,1},{1,0},{2,3},{3,2},{4,5},{5,4},{6,7},{7,6},{8,9},{9,8},{10,11... | collective-permute-start | bytes 172040 | tf_op jit(solution)/shard_map/ppermute | solution.py:324
  11.7 3.3 %collective-permute-start.2 = (bf16[32,896]{1,0:T(8,128)(2,1)S(1)}, bf16[32,896]{1,0:T(8,128)(2,1)S(1)}, u32[]{:S(2)}, u32[]{:S(2)}) collective-permute-start(bf16[32,896]{1,0:T(8,128)(2,1)S(1)} %collective-permute-done.1.refs_2_), channel_id=1, source_target_pairs={{0,1},{1,0},{2,3},{3,2},{4,5},{5,4},{6,7},{7,6},{8,9},{9,8},{10,11... | collective-permute-start | bytes 172040 | tf_op jit(solution)/shard_map/ppermute | solution.py:324
  15.0 17.1 %copy-start = (bf16[1536,768]{1,0:T(8,128)(2,1)S(1)}, bf16[1536,768]{1,0:T(8,128)(2,1)}, u32[]{:S(2)}) copy-start(bf16[1536,768]{1,0:T(8,128)(2,1)} %first_ref.3) | copy-start | bytes 7077892
  15.0 17.1 %copy-start.1 = (bf16[768,768]{1,0:T(8,128)(2,1)S(1)}, bf16[768,768]{1,0:T(8,128)(2,1)}, u32[]{:S(2)}) copy-start(bf16[768,768]{1,0:T(8,128)(2,1)} %second_ref.3) | copy-start | bytes 3538948
  15.1 17.1 %copy-start.5 = (bf16[1,16,768]{2,1,0:T(8,128)(2,1)S(1)}, bf16[1,16,768]{2,1,0:T(8,128)(2,1)}, u32[]{:S(2)}) copy-start(bf16[1,16,768]{2,1,0:T(8,128)(2,1)} %param.13) | copy-start | bytes 73732
  15.1 17.1 %copy-start.6 = (bf16[1,16,768]{2,1,0:T(8,128)(2,1)S(1)}, bf16[1,16,768]{2,1,0:T(8,128)(2,1)}, u32[]{:S(2)}) copy-start(bf16[1,16,768]{2,1,0:T(8,128)(2,1)} %param.14) | copy-start | bytes 73732
  15.1 17.0 %copy-start.7 = (f32[2,768]{1,0:T(2,128)S(1)}, f32[2,768]{1,0:T(2,128)}, u32[]{:S(2)}) copy-start(f32[2,768]{1,0:T(2,128)} %refs_7_.1) | copy-start | bytes 18436
  25.6 1.6 %collective-permute-start.7 = (bf16[1152,128]{1,0:T(8,128)(2,1)S(1)}, bf16[1152,128]{1,0:T(8,128)(2,1)S(1)}, u32[]{:S(2)}, u32[]{:S(2)}) collective-permute-start(bf16[1152,128]{1,0:T(8,128)(2,1)S(1)} %get-tuple-element.33.refs_0_), channel_id=1, source_target_pairs={{0,1},{1,0},{2,3},{3,2},{4,5},{5,4},{6,7},{7,6},{8,9},{9,8},{10,11... | collective-permute-start | bytes 884744 | tf_op jit(solution)/shard_map/ppermute | solution.py:324
  28.6 5.8 %collective-permute-start.8 = (bf16[80,768]{1,0:T(8,128)(2,1)S(1)}, bf16[80,768]{1,0:T(8,128)(2,1)S(1)}, u32[]{:S(2)}, u32[]{:S(2)}) collective-permute-start(bf16[80,768]{1,0:T(8,128)(2,1)S(1)} %get-tuple-element.43), channel_id=1, source_target_pairs={{0,8},{8,0},{16,24},{24,16},{1,9},{9,1},{17,25},{25,17},{2,10},{10... | collective-permute-start | bytes 368648 | tf_op jit(solution)/shard_map/ppermute | solution.py:324
  30.1 7.7 %collective-permute-start.9 = (bf16[80,768]{1,0:T(8,128)(2,1)S(1)}, bf16[80,768]{1,0:T(8,128)(2,1)S(1)}, u32[]{:S(2)}, u32[]{:S(2)}) collective-permute-start(bf16[80,768]{1,0:T(8,128)(2,1)S(1)} %get-tuple-element.44), channel_id=1, source_target_pairs={{0,16},{8,24},{16,0},{24,8},{1,17},{9,25},{17,1},{25,9},{2,18},{10... | collective-permute-start | bytes 368648 | tf_op jit(solution)/shard_map/ppermute | solution.py:324
  31.6 6.2 %collective-permute-start.10 = (bf16[80,768]{1,0:T(8,128)(2,1)S(1)}, bf16[80,768]{1,0:T(8,128)(2,1)S(1)}, u32[]{:S(2)}, u32[]{:S(2)}) collective-permute-start(bf16[80,768]{1,0:T(8,128)(2,1)S(1)} %get-tuple-element.45), channel_id=1, source_target_pairs={{0,24},{8,16},{16,8},{24,0},{1,25},{9,17},{17,9},{25,1},{2,26},{10... | collective-permute-start | bytes 368648 | tf_op jit(solution)/shard_map/ppermute | solution.py:324
  32.1 5.7 %copy-start.2 = (f32[55296]{0:T(1024)S(1)}, f32[55296]{0:T(1024)}, u32[]{:S(2)}) copy-start(f32[55296]{0:T(1024)} %param.21) | copy-start | bytes 663556
  32.1 5.7 %copy-start.3 = (f32[55296]{0:T(1024)S(1)}, f32[55296]{0:T(1024)}, u32[]{:S(2)}) copy-start(f32[55296]{0:T(1024)} %param.22) | copy-start | bytes 663556
  32.2 5.7 %copy-start.4 = (f32[55296]{0:T(1024)S(1)}, f32[55296]{0:T(1024)}, u32[]{:S(2)}) copy-start(f32[55296]{0:T(1024)} %param.23) | copy-start | bytes 663556
  32.2 5.7 %copy-start.8 = (f32[2,768]{1,0:T(2,128)S(1)}, f32[2,768]{1,0:T(2,128)}, u32[]{:S(2)}) copy-start(f32[2,768]{1,0:T(2,128)} %refs_8_.1) | copy-start | bytes 18436
  32.2 5.7 %copy-start.9 = (f32[2,768]{1,0:T(2,128)S(1)}, f32[2,768]{1,0:T(2,128)}, u32[]{:S(2)}) copy-start(f32[2,768]{1,0:T(2,128)} %refs_9_.1) | copy-start | bytes 18436
where the time goes:
time: 39.1 us; the launch traced here: 38.9 us
  Pallas kernels  18.6 us (48%)
  starting transfers between devices  9.92 us (25%)
  waiting for transfers between devices  9.47 us (24%)
  between operations  0.83 us (2%)
    pallas_call x6, Pallas kernels, call(): pl.pallas_call(body, out_shape=tuple(outs), in_specs=specs, out_specs=tup...  18.6 us
    ppermute x11, starting transfers between devices, swap(): return lax.ppermute(value, axis, [(i, i ^ distance) for i in range(count)])  9.92 us
    ppermute x11, waiting for transfers between devices, swap(): return lax.ppermute(value, axis, [(i, i ^ distance) for i in range(count)])  9.47 us
  transfers between devices with their start and end apart: 11, of which 4 were waited for; matrix products, arithmetic and copies ran while one was open for 0% of the time, Pallas kernels for 13%

commit v1 on v0

--- a/solution.py
+++ b/solution.py
@@ -87,31 +87,19 @@
     out_ref[rows:, rest:] = stacked.astype(BF16)
 
 
-def weight_kernel(split, place_ref, first_ref, second_ref, bias_ref, first_out, second_out, bias_out,
-                  held, second_held, bias_held, turned, sems):
-    features, part = second_ref.shape[1], second_out.shape[0]
-    wide, tall = held.shape[1], second_held.shape[0]
-    column = lax.rem(place_ref[0], split) * part
-    begin = pl.multiple_of(jnp.minimum(column // LANES * LANES, features - wide), LANES)
-    high = pl.multiple_of(jnp.minimum(column // 16 * 16, features - tall), 16)
-    columns = pl.ds(begin, wide)
+def weight_kernel(split, place_ref, first_ref, second_ref, bias_ref, *refs):
+    targets, sems = refs[:3], refs[3]
+    part = targets[1].shape[0]
+    mine = pl.ds(pl.multiple_of(lax.rem(place_ref[0], split) * part, LANES), part)
+    sources = [first_ref.at[:, mine], second_ref.at[mine, :], bias_ref.at[:, mine]]
     copies = [
-        pltpu.make_async_copy(first_ref.at[:, columns], held, sems.at[0]),
-        pltpu.make_async_copy(second_ref.at[pl.ds(high, tall), :], second_held, sems.at[1]),
-        pltpu.make_async_copy(bias_ref.at[:, columns], bias_held, sems.at[2]),
+        pltpu.make_async_copy(source, target, sems.at[i])
+        for i, (source, target) in enumerate(zip(sources, targets))
     ]
     for copy in copies:
         copy.start()
     for copy in copies:
         copy.wait()
-    mine = pl.ds(pl.multiple_of(column - begin, 8), part)
-    for i in range(2):
-        turned[...] = held[i * features : (i + 1) * features].astype(F32).T
-        first_out[i] = turned[mine, :].astype(BF16)
-    turned[:, :LANES] = jnp.broadcast_to(bias_held[:1, :], (LANES, wide)).T
-    bias_out[...] = turned[mine, :LANES]
-    turned[:tall, :] = second_held[...].astype(F32)
-    second_out[...] = turned[pl.ds(pl.multiple_of(column - high, 8), part), :].astype(BF16)
 
 
 def edge_kernel(scale, count, place_ref, *refs):
@@ -142,15 +130,13 @@
 
     nodes = nodes_ref[...]
     cot = cot_ref[...]
-    src_part = dot(first_ref[0], nodes, NT)
-    dst_part = dot(first_ref[1], nodes, NT) + bias_ref[:, :1]
+    src_part = dot(nodes, first_ref[:features], NN).T
+    dst_part = (dot(nodes, first_ref[features:], NN) + bias_ref[:1, :]).T
     cot_part = dot(second_ref[...], cot, NT)
 
-    src_high, src_low = split_two(0.5 * src_part)
-    dst_high, dst_low = split_two(0.5 * dst_part)
     cot_high, cot_low = split_two((0.5 * scale) * cot_part)
-    for i, piece in enumerate([src_high, dst_high, src_low, dst_low]):
-        left[:, i * node_total : (i + 1) * node_total] = piece
+    left[:, :node_total] = (0.5 * src_part).astype(BF16)
+    left[:, node_total:] = (0.5 * dst_part).astype(BF16)
     left_back[:, :node_total] = cot_high
     left_back[:, node_total:] = cot_low
     total[...] = jnp.zeros_like(total)
@@ -173,7 +159,7 @@
             weight = numbers[4:5] + numbers[5:6] + numbers[6:7]
         src_hot, dst_hot = one_hot(src), one_hot(dst)
         hot = jnp.concatenate([src_hot, dst_hot], 0)
-        halved = dot(left[...], jnp.concatenate([hot, hot], 0), NN)
+        halved = dot(left[...], hot, NN)
         back = dot(left_back[...], jnp.concatenate([dst_hot, dst_hot], 0), NN) * weight
         tilt = jnp.tanh(halved)
         rise = 1.0 + tilt
@@ -189,9 +175,9 @@
         return carry
 
     lax.fori_loop(0, edges.shape[0], body, 0, unroll=8 if quants == 4 else 1)
-    sums_ref[:part] = (scale * total[:part, node_total:]).astype(BF16)
-    sums_ref[part : 2 * part] = total[part : 2 * part, :node_total].astype(BF16)
-    sums_ref[2 * part :] = total[part : 2 * part, node_total:].astype(BF16)
+    sums_ref[:part] = scale * total[:part, node_total:]
+    sums_ref[part : 2 * part] = total[part : 2 * part, :node_total]
+    sums_ref[2 * part :] = total[part : 2 * part, node_total:]
     envelope = scale * (
         total[2 * part : 2 * part + 1, node_total:]
         + total[2 * part + 1 : 2 * part + 2, node_total:]
@@ -229,17 +215,17 @@
     slot = lax.rem(graph, split)
     for k in range(split):
         start = pl.multiple_of((slot ^ k) * part, 8)
-        block = blocks[k][...].astype(F32)
+        block = blocks[k][...]
         left[pl.ds(pl.multiple_of(2 * features + start, 8), part), :] = block[:part]
         src_sum[pl.ds(start, part), :] = block[part : 2 * part]
         dst_sum[pl.ds(start, part), :] = block[2 * part :]
 
-    src_all = src_sum[...].astype(BF16)
-    dst_all = dst_sum[...].astype(BF16)
+    src_all = jnp.concatenate(split_two(src_sum[...]), 1)
+    dst_all = jnp.concatenate(split_two(dst_sum[...]), 1)
     cot = cot_ref[...]
-    active_ref[...] = left[2 * features : 3 * features].astype(BF16)
-    src_ref[...] = src_all
-    dst_ref[...] = dst_all
+    active_ref[...] = left[2 * features : 3 * features]
+    src_ref[...] = src_sum[...]
+    dst_ref[...] = dst_sum[...]
 
     kinds = []
     rows = []
@@ -252,8 +238,12 @@
     zero = jnp.zeros_like(rows)
     from_src = jnp.where(kinds < features, rows, zero).astype(BF16)
     from_dst = jnp.where((kinds >= features) & (kinds < 2 * features), rows, zero).astype(BF16)
-    from_act = jnp.where(kinds >= 2 * features, rows, zero).astype(BF16)
-    grads = dot(from_src, src_all, NT) + dot(from_dst, dst_all, NT) + dot(from_act, cot, NN)
+    from_act = jnp.concatenate(split_two(jnp.where(kinds >= 2 * features, rows, zero)), 1)
+    grads = (
+        dot(jnp.concatenate([from_src, from_src], 1), src_all, NT)
+        + dot(jnp.concatenate([from_dst, from_dst], 1), dst_all, NT)
+        + dot(from_act, jnp.concatenate([cot, cot], 0), NN)
+    )
 
     ones = jnp.ones((8, dst_all.shape[1]), BF16)
     bias_pre = dot(ones, dst_all, NT)[:1]
@@ -278,8 +268,12 @@
     at = pl.ds(pl.multiple_of(place_ref[0] * rows, rows), rows)
 
     def own(ref):
-        wide[...] = ref[...].astype(F32).T
-        return wide[at, :].astype(BF16)
+        wide[...] = ref[...].T
+        return jnp.concatenate(split_two(wide[at, :]), 0)
+
+    def both(value, weight, dims):
+        result = dot(value, weight, dims)
+        return result[:rows] + result[rows:]
 
     active = own(active_ref)
     src = own(src_ref)
@@ -288,9 +282,9 @@
     column = jnp.broadcast_to(env[:1], (node_total, node_total)).T
     wide[:, :node_total] = column
     env_own = wide[at, :1]
-    summed = dot(active, second_ref[...], NN) + env_own * bias_ref[1:2, :]
+    summed = both(active, second_ref[...], NN) + env_own * bias_ref[1:2, :]
     out_ref[...] = (nodes_ref[...].astype(F32) + summed).astype(BF16)
-    back = dot(src, first_ref[:features], NT) + dot(dst, first_ref[features:], NT)
+    back = both(src, first_ref[:features], NT) + both(dst, first_ref[features:], NT)
     grad_ref[...] = cot_ref[...].astype(F32) + back
 
 
@@ -392,9 +386,6 @@
     graph = lax.axis_index("graph")
     group = lax.axis_index("dp")
 
-    over = max(i * part % LANES for i in range(split))
-    wide = min(features, -(-(part + over) // LANES) * LANES)
-    tall = min(features, part if part % 16 == 0 else -(-part // 16) * 16 + 16)
     place = jnp.stack([graph, group]).astype(jnp.int32)
 
     quants = 4 if node_total <= EXACT else 8
@@ -413,17 +404,11 @@
         functools.partial(weight_kernel, split),
         [w_first, w_second, biases],
         [
-            struct((2, part, features), BF16),
+            struct((2 * features, part), BF16),
             struct((part, features), BF16),
-            struct((part, LANES), F32),
+            struct((2, part), F32),
         ],
-        [
-            pltpu.VMEM((2 * features, wide), BF16),
-            pltpu.VMEM((tall, features), BF16),
-            pltpu.VMEM((2, wide), F32),
-            pltpu.VMEM((wide, features), F32),
-            pltpu.SemaphoreType.DMA((3,)),
-        ],
+        [pltpu.SemaphoreType.DMA((3,))],
         place=place,
         far=range(3),
     )
@@ -431,13 +416,13 @@
         functools.partial(edge_kernel, scale, count),
         blocks + list(weights),
         [
-            struct((3 * part, node_total), BF16),
+            struct((3 * part, node_total), F32),
             struct((8, node_total), F32),
             struct((node_total, features), BF16),
             struct((node_total, features), BF16),
         ],
         [
-            pltpu.VMEM((part, 4 * node_total), BF16),
+            pltpu.VMEM((part, 2 * node_total), BF16),
             pltpu.VMEM((part, 2 * node_total), BF16),
             pltpu.VMEM((count, quants, edge_count), F32),
             pltpu.VMEM((2 * part + 16, 2 * node_total), F32),
@@ -452,7 +437,7 @@
         blocks + [all_nodes, all_cot, envelope],
         [struct((tall, features), F32)]
         + [struct((tall, features), BF16)] * (groups - 1)
-        + [struct((features, node_total), BF16)] * 3,
+        + [struct((features, node_total), F32)] * 3,
         [
             pltpu.VMEM((3 * features + 16, node_total), F32),
             pltpu.VMEM((features, node_total), F32),

time: 39.1 us -> 37.3 us (0.954)
  Pallas kernels: 18.6 us -> 16.4 us
    pallas_call x6, Pallas kernels: 18.6 us -> 16.4 us  [call(): pl.pallas_call(body, out_shape=tuple(outs), in_specs=specs, out_specs=tup...]
  transfers between devices with their start and end apart: 11 -> 11, of which waited for: 4 -> 4; matrix products, arithmetic and copies ran while one was open for 0% -> 0% of each run, Pallas kernels for 13% -> 11%
where the time goes in v1:
time: 37.3 us; the launch traced here: 37.1 us
  Pallas kernels  16.4 us (44%)
  starting transfers between devices  9.92 us (27%)
  waiting for transfers between devices  9.83 us (26%)
  between operations  0.83 us (2%)
    pallas_call x6, Pallas kernels, call(): pl.pallas_call(body, out_shape=tuple(outs), in_specs=specs, out_specs=tup...  16.4 us
    ppermute x11, starting transfers between devices, swap(): return lax.ppermute(value, axis, [(i, i ^ distance) for i in range(count)])  9.92 us
    ppermute x11, waiting for transfers between devices, swap(): return lax.ppermute(value, axis, [(i, i ^ distance) for i in range(count)])  9.83 us
  transfers between devices with their start and end apart: 11, of which 4 were waited for; matrix products, arithmetic and copies ran while one was open for 0% of the time, Pallas kernels for 11%

profile of v1, /device:TPU:0, one launch (start us, length us, event | category | flops | bytes accessed | tf_op | source)
XLA Modules:
  0.0 37.1 jit_solution(1306531907376090144)
XLA Ops:
  0.6 0.8 %shard_map.188.refs_0_ = bf16[32,896]{1,0:T(8,128)(2,1)S(1)} custom-call(bf16[16,768]{1,0:T(8,128)(2,1)} %bitcast.15, bf16[16,768]{1,0:T(8,128)(2,1)} %bitcast.17, s32[1,1024]{1,0:T(1,128)} %refs_2_.1, s32[1,1024]{1,0:T(1,128)} %refs_3_.1, f32[1,1024]{1,0:T(1,128)} %refs_4_.1), custom_call_target="tpu_custom_call" | custom-call | bytes 118784 | tf_op jit(solution)/shard_map/pallas_call | solution.py:349
  1.5 5.1 %collective-permute-start.5 = (bf16[32,896]{1,0:T(8,128)(2,1)S(1)}, bf16[32,896]{1,0:T(8,128)(2,1)S(1)}, u32[]{:S(2)}, u32[]{:S(2)}) collective-permute-start(bf16[32,896]{1,0:T(8,128)(2,1)S(1)} %shard_map.188.refs_0_), channel_id=1, source_target_pairs={{0,6},{1,7},{2,4},{3,5},{4,2},{5,3},{6,0},{7,1},{8,14},{9,15},{10,... | collective-permute-start | bytes 172040 | tf_op jit(solution)/shard_map/ppermute | solution.py:318
  6.6 0.0 collective-permute-start.3
  6.6 0.6 %collective-permute-start.1 = (bf16[32,896]{1,0:T(8,128)(2,1)S(1)}, bf16[32,896]{1,0:T(8,128)(2,1)S(1)}, u32[]{:S(2)}, u32[]{:S(2)}) collective-permute-start(bf16[32,896]{1,0:T(8,128)(2,1)S(1)} %shard_map.188.refs_0_), channel_id=1, source_target_pairs={{0,2},{1,3},{2,0},{3,1},{4,6},{5,7},{6,4},{7,5},{8,10},{9,11},{10,... | collective-permute-start | bytes 172040 | tf_op jit(solution)/shard_map/ppermute | solution.py:318
  7.3 0.0 collective-permute-start
  7.3 1.7 %collective-permute-done.5.refs_6_ = bf16[32,896]{1,0:T(8,128)(2,1)S(1)} collective-permute-done((bf16[32,896]{1,0:T(8,128)(2,1)S(1)}, bf16[32,896]{1,0:T(8,128)(2,1)S(1)}, u32[]{:S(2)}, u32[]{:S(2)}) %collective-permute-start.5) | collective-permute-done | bytes 57376 | tf_op jit(solution)/shard_map/ppermute | solution.py:318
  8.9 0.0 collective-permute-start.6
  8.9 2.8 %collective-permute-done.3.refs_4_ = bf16[32,896]{1,0:T(8,128)(2,1)S(1)} collective-permute-done((bf16[32,896]{1,0:T(8,128)(2,1)S(1)}, bf16[32,896]{1,0:T(8,128)(2,1)S(1)}, u32[]{:S(2)}, u32[]{:S(2)}) %collective-permute-start.3) | collective-permute-done | bytes 57376 | tf_op jit(solution)/shard_map/ppermute | solution.py:318
  11.7 0.0 collective-permute-start.4
  11.7 0.0 collective-permute-done.1.refs_2_
  11.7 0.5 %collective-permute-start.2 = (bf16[32,896]{1,0:T(8,128)(2,1)S(1)}, bf16[32,896]{1,0:T(8,128)(2,1)S(1)}, u32[]{:S(2)}, u32[]{:S(2)}) collective-permute-start(bf16[32,896]{1,0:T(8,128)(2,1)S(1)} %collective-permute-done.1.refs_2_), channel_id=1, source_target_pairs={{0,1},{1,0},{2,3},{3,2},{4,5},{5,4},{6,7},{7,6},{8,9},{9,8},{10,11... | collective-permute-start | bytes 172040 | tf_op jit(solution)/shard_map/ppermute | solution.py:318
  12.2 0.1 pad_add_fusion.place_ref
  12.3 2.0 %shard_map.189 = (bf16[1536,384]{1,0:T(8,128)(2,1)S(1)}, bf16[384,768]{1,0:T(8,128)(2,1)S(1)}, f32[2,384]{1,0:T(2,128)S(1)}) custom-call(s32[2]{0:T(128)S(1)} %pad_add_fusion.place_ref, bf16[1536,768]{1,0:T(8,128)(2,1)} %first_ref.3, bf16[768,768]{1,0:T(8,128)(2,1)} %second_ref.3, f32[2,768]{1,0:T(2,128)} %refs_7_.1), custom_call_target="tpu_custom_call" | custom-call | bytes 5317632 | tf_op jit(solution)/shard_map/pallas_call | solution.py:349
  14.3 0.0 collective-permute-done.refs_1_
  14.3 0.0 collective-permute-done.6.refs_7_
  14.3 0.0 collective-permute-done.4.refs_5_
  14.3 0.0 collective-permute-done.2.refs_3_
  14.3 0.0 copy-start
  14.3 8.9 %shard_map.190 = (f32[1152,128]{1,0:T(8,128)S(1)}, f32[8,128]{1,0:T(8,128)S(1)}, bf16[128,768]{1,0:T(8,128)(2,1)S(1)}, bf16[128,768]{1,0:T(8,128)(2,1)S(1)}) custom-call(s32[2]{0:T(128)S(1)} %pad_add_fusion.place_ref, bf16[32,896]{1,0:T(8,128)(2,1)S(1)} %shard_map.188.refs_0_, bf16[32,896]{1,0:T(8,128)(2,1)S(1)} %collective-permute-done.refs_1_, ...), custom_call_target="tpu_custom_call" | custom-call | flops 6442450944 | bytes 3218432 | tf_op jit(solution)/shard_map/pallas_call | solution.py:349
  23.2 0.0 copy-start.1
  23.2 0.0 copy-start.5
  23.2 0.0 copy-start.6
  23.2 0.0 copy-start.7
  23.2 0.1 collective-permute-start.7
  23.3 2.0 %collective-permute-done.7.refs_1_ = f32[1152,128]{1,0:T(8,128)S(1)} collective-permute-done((f32[1152,128]{1,0:T(8,128)S(1)}, f32[1152,128]{1,0:T(8,128)S(1)}, u32[]{:S(2)}, u32[]{:S(2)}) %collective-permute-start.7) | collective-permute-done | bytes 589856 | tf_op jit(solution)/shard_map/ppermute | solution.py:318
  25.3 1.4 %shard_map.191 = (f32[80,768]{1,0:T(8,128)S(1)}, bf16[80,768]{1,0:T(8,128)(2,1)S(1)}, bf16[80,768]{1,0:T(8,128)(2,1)S(1)}, bf16[80,768]{1,0:T(8,128)(2,1)S(1)}, ...) custom-call(s32[2]{0:T(128)S(1)} %pad_add_fusion.place_ref, ...), custom_call_target="tpu_custom_call" | custom-call | flops 169869312 | bytes 3371008 | tf_op jit(solution)/shard_map/pallas_call | solution.py:349
  26.7 1.6 %collective-permute-start.8 = (bf16[80,768]{1,0:T(8,128)(2,1)S(1)}, bf16[80,768]{1,0:T(8,128)(2,1)S(1)}, u32[]{:S(2)}, u32[]{:S(2)}) collective-permute-start(bf16[80,768]{1,0:T(8,128)(2,1)S(1)} %get-tuple-element.43), channel_id=1, source_target_pairs={{0,8},{8,0},{16,24},{24,16},{1,9},{9,1},{17,25},{25,17},{2,10},{10... | collective-permute-start | bytes 368648 | tf_op jit(solution)/shard_map/ppermute | solution.py:318
  28.3 1.5 %collective-permute-start.9 = (bf16[80,768]{1,0:T(8,128)(2,1)S(1)}, bf16[80,768]{1,0:T(8,128)(2,1)S(1)}, u32[]{:S(2)}, u32[]{:S(2)}) collective-permute-start(bf16[80,768]{1,0:T(8,128)(2,1)S(1)} %get-tuple-element.44), channel_id=1, source_target_pairs={{0,16},{8,24},{16,0},{24,8},{1,17},{9,25},{17,1},{25,9},{2,18},{10... | collective-permute-start | bytes 368648 | tf_op jit(solution)/shard_map/ppermute | solution.py:318
  29.8 0.5 %collective-permute-start.10 = (bf16[80,768]{1,0:T(8,128)(2,1)S(1)}, bf16[80,768]{1,0:T(8,128)(2,1)S(1)}, u32[]{:S(2)}, u32[]{:S(2)}) collective-permute-start(bf16[80,768]{1,0:T(8,128)(2,1)S(1)} %get-tuple-element.45), channel_id=1, source_target_pairs={{0,24},{8,16},{16,8},{24,0},{1,25},{9,17},{17,9},{25,1},{2,26},{10... | collective-permute-start | bytes 368648 | tf_op jit(solution)/shard_map/ppermute | solution.py:318
  30.3 0.0 copy-done
  30.3 0.0 copy-done.1
  30.3 0.0 copy-done.5
  30.3 0.0 copy-done.6
  30.3 0.0 copy-done.7
  30.3 0.0 copy-start.2
  30.3 0.0 copy-start.3
  30.3 0.0 copy-start.4
  30.3 0.0 copy-start.8
  30.3 0.0 copy-start.9
  30.4 2.2 %shard_map.192 = (bf16[16,768]{1,0:T(8,128)(2,1)}, f32[16,768]{1,0:T(8,128)}) custom-call(s32[2]{0:T(128)S(1)} %pad_add_fusion.place_ref, f32[768,128]{1,0:T(8,128)S(1)} %get-tuple-element.37.active_ref, f32[768,128]{1,0:T(8,128)S(1)} %get-tuple-element.38.src_ref, f32[768,128]{1,0:T(8,128)S(1)} %get-tuple-element.39.dst_ref, ...), custom_call_target="tpu_custom_call" | custom-call | flops 452984832 | bytes 4851712 | tf_op jit(solution)/shard_map/pallas_call | solution.py:349
  32.6 0.0 collective-permute-done.8.refs_1_
  32.6 3.4 %collective-permute-done.9.refs_2_ = bf16[80,768]{1,0:T(8,128)(2,1)S(1)} collective-permute-done((bf16[80,768]{1,0:T(8,128)(2,1)S(1)}, bf16[80,768]{1,0:T(8,128)(2,1)S(1)}, u32[]{:S(2)}, u32[]{:S(2)}) %collective-permute-start.9) | collective-permute-done | bytes 122912 | tf_op jit(solution)/shard_map/ppermute | solution.py:318
  36.0 0.0 collective-permute-done.10.refs_3_
  36.0 0.0 copy-done.2
  36.0 0.0 copy-done.3
  36.0 0.0 copy-done.4
  36.0 0.0 copy-done.8
  36.0 1.1 %shard_map.193 = (f32[432,128]{1,0:T(8,128)}, f32[432,128]{1,0:T(8,128)}, f32[432,128]{1,0:T(8,128)}, f32[2,768]{1,0:T(2,128)}, f32[2,768]{1,0:T(2,128)}, /*index=5*/f32[2,768]{1,0:T(2,128)}) custom-call(f32[80,768]{1,0:T(8,128)S(1)} %get-tuple-element.42.refs_0_, bf16[80,768]{1,0:T(8,128)(2,1)S(1)} %collective-permute-done.8.refs_1_, ...), custom_call_target="tpu_custom_call" | custom-call | bytes 1978368 | tf_op jit(solution)/shard_map/pallas_call | solution.py:349
  (1 shorter events, 0.0 us)
Async XLA Ops:
  1.5 7.5 %collective-permute-start.5 = (bf16[32,896]{1,0:T(8,128)(2,1)S(1)}, bf16[32,896]{1,0:T(8,128)(2,1)S(1)}, u32[]{:S(2)}, u32[]{:S(2)}) collective-permute-start(bf16[32,896]{1,0:T(8,128)(2,1)S(1)} %shard_map.188.refs_0_), channel_id=1, source_target_pairs={{0,6},{1,7},{2,4},{3,5},{4,2},{5,3},{6,0},{7,1},{8,14},{9,15},{10,... | collective-permute-start | bytes 172040 | tf_op jit(solution)/shard_map/ppermute | solution.py:318
  6.6 5.1 %collective-permute-start.3 = (bf16[32,896]{1,0:T(8,128)(2,1)S(1)}, bf16[32,896]{1,0:T(8,128)(2,1)S(1)}, u32[]{:S(2)}, u32[]{:S(2)}) collective-permute-start(bf16[32,896]{1,0:T(8,128)(2,1)S(1)} %shard_map.188.refs_0_), channel_id=1, source_target_pairs={{0,4},{1,5},{2,6},{3,7},{4,0},{5,1},{6,2},{7,3},{8,12},{9,13},{10,... | collective-permute-start | bytes 172040 | tf_op jit(solution)/shard_map/ppermute | solution.py:318
  6.6 5.1 %collective-permute-start.1 = (bf16[32,896]{1,0:T(8,128)(2,1)S(1)}, bf16[32,896]{1,0:T(8,128)(2,1)S(1)}, u32[]{:S(2)}, u32[]{:S(2)}) collective-permute-start(bf16[32,896]{1,0:T(8,128)(2,1)S(1)} %shard_map.188.refs_0_), channel_id=1, source_target_pairs={{0,2},{1,3},{2,0},{3,1},{4,6},{5,7},{6,4},{7,5},{8,10},{9,11},{10,... | collective-permute-start | bytes 172040 | tf_op jit(solution)/shard_map/ppermute | solution.py:318
  7.3 7.0 %collective-permute-start = (bf16[32,896]{1,0:T(8,128)(2,1)S(1)}, bf16[32,896]{1,0:T(8,128)(2,1)S(1)}, u32[]{:S(2)}, u32[]{:S(2)}) collective-permute-start(bf16[32,896]{1,0:T(8,128)(2,1)S(1)} %shard_map.188.refs_0_), channel_id=1, source_target_pairs={{0,1},{1,0},{2,3},{3,2},{4,5},{5,4},{6,7},{7,6},{8,9},{9,8},{10,11... | collective-permute-start | bytes 172040 | tf_op jit(solution)/shard_map/ppermute | solution.py:318
  8.9 5.4 %collective-permute-start.6 = (bf16[32,896]{1,0:T(8,128)(2,1)S(1)}, bf16[32,896]{1,0:T(8,128)(2,1)S(1)}, u32[]{:S(2)}, u32[]{:S(2)}) collective-permute-start(bf16[32,896]{1,0:T(8,128)(2,1)S(1)} %collective-permute-done.5.refs_6_), channel_id=1, source_target_pairs={{0,1},{1,0},{2,3},{3,2},{4,5},{5,4},{6,7},{7,6},{8,9},{9,8},{10,11... | collective-permute-start | bytes 172040 | tf_op jit(solution)/shard_map/ppermute | solution.py:318
  11.7 2.6 %collective-permute-start.4 = (bf16[32,896]{1,0:T(8,128)(2,1)S(1)}, bf16[32,896]{1,0:T(8,128)(2,1)S(1)}, u32[]{:S(2)}, u32[]{:S(2)}) collective-permute-start(bf16[32,896]{1,0:T(8,128)(2,1)S(1)} %collective-permute-done.3.refs_4_), channel_id=1, source_target_pairs={{0,1},{1,0},{2,3},{3,2},{4,5},{5,4},{6,7},{7,6},{8,9},{9,8},{10,11... | collective-permute-start | bytes 172040 | tf_op jit(solution)/shard_map/ppermute | solution.py:318
  11.7 2.6 %collective-permute-start.2 = (bf16[32,896]{1,0:T(8,128)(2,1)S(1)}, bf16[32,896]{1,0:T(8,128)(2,1)S(1)}, u32[]{:S(2)}, u32[]{:S(2)}) collective-permute-start(bf16[32,896]{1,0:T(8,128)(2,1)S(1)} %collective-permute-done.1.refs_2_), channel_id=1, source_target_pairs={{0,1},{1,0},{2,3},{3,2},{4,5},{5,4},{6,7},{7,6},{8,9},{9,8},{10,11... | collective-permute-start | bytes 172040 | tf_op jit(solution)/shard_map/ppermute | solution.py:318
  14.3 16.0 %copy-start = (bf16[1536,768]{1,0:T(8,128)(2,1)S(1)}, bf16[1536,768]{1,0:T(8,128)(2,1)}, u32[]{:S(2)}) copy-start(bf16[1536,768]{1,0:T(8,128)(2,1)} %first_ref.3) | copy-start | bytes 7077892
  23.2 7.1 %copy-start.1 = (bf16[768,768]{1,0:T(8,128)(2,1)S(1)}, bf16[768,768]{1,0:T(8,128)(2,1)}, u32[]{:S(2)}) copy-start(bf16[768,768]{1,0:T(8,128)(2,1)} %second_ref.3) | copy-start | bytes 3538948
  23.2 7.1 %copy-start.5 = (bf16[1,16,768]{2,1,0:T(8,128)(2,1)S(1)}, bf16[1,16,768]{2,1,0:T(8,128)(2,1)}, u32[]{:S(2)}) copy-start(bf16[1,16,768]{2,1,0:T(8,128)(2,1)} %param.13) | copy-start | bytes 73732
  23.2 7.1 %copy-start.6 = (bf16[1,16,768]{2,1,0:T(8,128)(2,1)S(1)}, bf16[1,16,768]{2,1,0:T(8,128)(2,1)}, u32[]{:S(2)}) copy-start(bf16[1,16,768]{2,1,0:T(8,128)(2,1)} %param.14) | copy-start | bytes 73732
  23.2 7.1 %copy-start.7 = (f32[2,768]{1,0:T(2,128)S(1)}, f32[2,768]{1,0:T(2,128)}, u32[]{:S(2)}) copy-start(f32[2,768]{1,0:T(2,128)} %refs_7_.1) | copy-start | bytes 18436
  23.2 2.1 %collective-permute-start.7 = (f32[1152,128]{1,0:T(8,128)S(1)}, f32[1152,128]{1,0:T(8,128)S(1)}, u32[]{:S(2)}, u32[]{:S(2)}) collective-permute-start(f32[1152,128]{1,0:T(8,128)S(1)} %get-tuple-element.33.refs_0_), channel_id=1, source_target_pairs={{0,1},{1,0},{2,3},{3,2},{4,5},{5,4},{6,7},{7,6},{8,9},{9,8},{10,11... | collective-permute-start | bytes 1769480 | tf_op jit(solution)/shard_map/ppermute | solution.py:318
  26.7 5.9 %collective-permute-start.8 = (bf16[80,768]{1,0:T(8,128)(2,1)S(1)}, bf16[80,768]{1,0:T(8,128)(2,1)S(1)}, u32[]{:S(2)}, u32[]{:S(2)}) collective-permute-start(bf16[80,768]{1,0:T(8,128)(2,1)S(1)} %get-tuple-element.43), channel_id=1, source_target_pairs={{0,8},{8,0},{16,24},{24,16},{1,9},{9,1},{17,25},{25,17},{2,10},{10... | collective-permute-start | bytes 368648 | tf_op jit(solution)/shard_map/ppermute | solution.py:318
  28.3 7.7 %collective-permute-start.9 = (bf16[80,768]{1,0:T(8,128)(2,1)S(1)}, bf16[80,768]{1,0:T(8,128)(2,1)S(1)}, u32[]{:S(2)}, u32[]{:S(2)}) collective-permute-start(bf16[80,768]{1,0:T(8,128)(2,1)S(1)} %get-tuple-element.44), channel_id=1, source_target_pairs={{0,16},{8,24},{16,0},{24,8},{1,17},{9,25},{17,1},{25,9},{2,18},{10... | collective-permute-start | bytes 368648 | tf_op jit(solution)/shard_map/ppermute | solution.py:318
  29.8 6.2 %collective-permute-start.10 = (bf16[80,768]{1,0:T(8,128)(2,1)S(1)}, bf16[80,768]{1,0:T(8,128)(2,1)S(1)}, u32[]{:S(2)}, u32[]{:S(2)}) collective-permute-start(bf16[80,768]{1,0:T(8,128)(2,1)S(1)} %get-tuple-element.45), channel_id=1, source_target_pairs={{0,24},{8,16},{16,8},{24,0},{1,25},{9,17},{17,9},{25,1},{2,26},{10... | collective-permute-start | bytes 368648 | tf_op jit(solution)/shard_map/ppermute | solution.py:318
  30.3 5.7 %copy-start.2 = (f32[55296]{0:T(1024)S(1)}, f32[55296]{0:T(1024)}, u32[]{:S(2)}) copy-start(f32[55296]{0:T(1024)} %param.21) | copy-start | bytes 663556
  30.3 5.7 %copy-start.3 = (f32[55296]{0:T(1024)S(1)}, f32[55296]{0:T(1024)}, u32[]{:S(2)}) copy-start(f32[55296]{0:T(1024)} %param.22) | copy-start | bytes 663556
  30.3 5.7 %copy-start.4 = (f32[55296]{0:T(1024)S(1)}, f32[55296]{0:T(1024)}, u32[]{:S(2)}) copy-start(f32[55296]{0:T(1024)} %param.23) | copy-start | bytes 663556
  30.3 5.7 %copy-start.8 = (f32[2,768]{1,0:T(2,128)S(1)}, f32[2,768]{1,0:T(2,128)}, u32[]{:S(2)}) copy-start(f32[2,768]{1,0:T(2,128)} %refs_8_.1) | copy-start | bytes 18436
  30.3 5.7 %copy-start.9 = (f32[2,768]{1,0:T(2,128)S(1)}, f32[2,768]{1,0:T(2,128)}, u32[]{:S(2)}) copy-start(f32[2,768]{1,0:T(2,128)} %refs_9_.1) | copy-start | bytes 18436

commit v2 on v1

--- a/solution.py
+++ b/solution.py
@@ -126,7 +126,7 @@
         cot_ref[at, beside:] = blocks[k][rows:, :rest]
         numbers = blocks[k][rows:, rest:].astype(F32)
         for i in range(pieces):
-            edges[k, :, i * half : (i + 1) * half] = numbers[i * quants : (i + 1) * quants]
+            edges[graph ^ k, :, i * half : (i + 1) * half] = numbers[i * quants : (i + 1) * quants]
 
     nodes = nodes_ref[...]
     cot = cot_ref[...]
@@ -249,12 +249,12 @@
     bias_pre = dot(ones, dst_all, NT)[:1]
     env_high, env_low = split_two(envelope_ref[...])
     bias_out = (dot(env_high, cot, NN) + dot(env_low, cot, NN))[:1]
-    pre_high = bias_pre.astype(BF16).astype(F32)
-    out_high = bias_out.astype(BF16).astype(F32)
+    pre_high, pre_low = [piece.astype(F32) for piece in split_two(bias_pre)]
+    out_high, out_low = [piece.astype(F32) for piece in split_two(bias_out)]
     tail = outs[0].shape[0] - share
     pad = jnp.zeros((tail - 4, features), F32)
     extra = jnp.concatenate(
-        [pre_high, bias_pre - pre_high, out_high, bias_out - out_high, pad], 0
+        [pre_high, pre_low, out_high, out_low, pad], 0
     )
     for k in range(groups):
         full = jnp.concatenate([grads[k * share : (k + 1) * share], extra], 0)
@@ -296,10 +296,10 @@
     outs = refs[groups + 6 : groups + 12]
     flat = refs[groups + 12]
     features = parts[0].shape[1]
-    total = parts[0][...]
-    for ref in parts[1:]:
-        total = total + ref[...].astype(F32)
-    total = total * (1.0 / groups)
+    sums = [ref[...].astype(F32) for ref in parts]
+    while len(sums) > 1:
+        sums = [a + b for a, b in zip(sums[::2], sums[1::2])]
+    total = sums[0] * (1.0 / groups)
     across = features // LANES
     share = flat.shape[0] // across
     for q in range(across):

time: 37.3 us -> 37.3 us (level)
  no operation moved by 1% of the time
where the time goes in v2:
time: 37.3 us; the launch traced here: 37.1 us
  Pallas kernels  16.4 us (44%)
  starting transfers between devices  9.93 us (27%)
  waiting for transfers between devices  9.83 us (26%)
  between operations  0.83 us (2%)
    pallas_call x6, Pallas kernels, call(): pl.pallas_call(body, out_shape=tuple(outs), in_specs=specs, out_specs=tup...  16.4 us
    ppermute x11, starting transfers between devices, swap(): return lax.ppermute(value, axis, [(i, i ^ distance) for i in range(count)])  9.93 us
    ppermute x11, waiting for transfers between devices, swap(): return lax.ppermute(value, axis, [(i, i ^ distance) for i in range(count)])  9.83 us
  transfers between devices with their start and end apart: 11, of which 4 were waited for; matrix products, arithmetic and copies ran while one was open for 0% of the time, Pallas kernels for 11%

profile of v2, /device:TPU:0, one launch (start us, length us, event | category | flops | bytes accessed | tf_op | source)
XLA Modules:
  0.0 37.1 jit_solution(16013536073602384710)
XLA Ops:
  0.6 0.8 %shard_map.188.refs_0_ = bf16[32,896]{1,0:T(8,128)(2,1)S(1)} custom-call(bf16[16,768]{1,0:T(8,128)(2,1)} %bitcast.15, bf16[16,768]{1,0:T(8,128)(2,1)} %bitcast.17, s32[1,1024]{1,0:T(1,128)} %refs_2_.1, s32[1,1024]{1,0:T(1,128)} %refs_3_.1, f32[1,1024]{1,0:T(1,128)} %refs_4_.1), custom_call_target="tpu_custom_call" | custom-call | bytes 118784 | tf_op jit(solution)/shard_map/pallas_call | solution.py:349
  1.5 5.1 %collective-permute-start.5 = (bf16[32,896]{1,0:T(8,128)(2,1)S(1)}, bf16[32,896]{1,0:T(8,128)(2,1)S(1)}, u32[]{:S(2)}, u32[]{:S(2)}) collective-permute-start(bf16[32,896]{1,0:T(8,128)(2,1)S(1)} %shard_map.188.refs_0_), channel_id=1, source_target_pairs={{0,6},{1,7},{2,4},{3,5},{4,2},{5,3},{6,0},{7,1},{8,14},{9,15},{10,... | collective-permute-start | bytes 172040 | tf_op jit(solution)/shard_map/ppermute | solution.py:318
  6.6 0.0 collective-permute-start.3
  6.6 0.6 %collective-permute-start.1 = (bf16[32,896]{1,0:T(8,128)(2,1)S(1)}, bf16[32,896]{1,0:T(8,128)(2,1)S(1)}, u32[]{:S(2)}, u32[]{:S(2)}) collective-permute-start(bf16[32,896]{1,0:T(8,128)(2,1)S(1)} %shard_map.188.refs_0_), channel_id=1, source_target_pairs={{0,2},{1,3},{2,0},{3,1},{4,6},{5,7},{6,4},{7,5},{8,10},{9,11},{10,... | collective-permute-start | bytes 172040 | tf_op jit(solution)/shard_map/ppermute | solution.py:318
  7.3 0.0 collective-permute-start
  7.3 1.7 %collective-permute-done.5.refs_6_ = bf16[32,896]{1,0:T(8,128)(2,1)S(1)} collective-permute-done((bf16[32,896]{1,0:T(8,128)(2,1)S(1)}, bf16[32,896]{1,0:T(8,128)(2,1)S(1)}, u32[]{:S(2)}, u32[]{:S(2)}) %collective-permute-start.5) | collective-permute-done | bytes 57376 | tf_op jit(solution)/shard_map/ppermute | solution.py:318
  8.9 0.0 collective-permute-start.6
  8.9 2.8 %collective-permute-done.3.refs_4_ = bf16[32,896]{1,0:T(8,128)(2,1)S(1)} collective-permute-done((bf16[32,896]{1,0:T(8,128)(2,1)S(1)}, bf16[32,896]{1,0:T(8,128)(2,1)S(1)}, u32[]{:S(2)}, u32[]{:S(2)}) %collective-permute-start.3) | collective-permute-done | bytes 57376 | tf_op jit(solution)/shard_map/ppermute | solution.py:318
  11.7 0.0 collective-permute-start.4
  11.7 0.0 collective-permute-done.1.refs_2_
  11.7 0.5 %collective-permute-start.2 = (bf16[32,896]{1,0:T(8,128)(2,1)S(1)}, bf16[32,896]{1,0:T(8,128)(2,1)S(1)}, u32[]{:S(2)}, u32[]{:S(2)}) collective-permute-start(bf16[32,896]{1,0:T(8,128)(2,1)S(1)} %collective-permute-done.1.refs_2_), channel_id=1, source_target_pairs={{0,1},{1,0},{2,3},{3,2},{4,5},{5,4},{6,7},{7,6},{8,9},{9,8},{10,11... | collective-permute-start | bytes 172040 | tf_op jit(solution)/shard_map/ppermute | solution.py:318
  12.2 0.1 pad_add_fusion.place_ref
  12.3 2.0 %shard_map.189 = (bf16[1536,384]{1,0:T(8,128)(2,1)S(1)}, bf16[384,768]{1,0:T(8,128)(2,1)S(1)}, f32[2,384]{1,0:T(2,128)S(1)}) custom-call(s32[2]{0:T(128)S(1)} %pad_add_fusion.place_ref, bf16[1536,768]{1,0:T(8,128)(2,1)} %first_ref.3, bf16[768,768]{1,0:T(8,128)(2,1)} %second_ref.3, f32[2,768]{1,0:T(2,128)} %refs_7_.1), custom_call_target="tpu_custom_call" | custom-call | bytes 5317632 | tf_op jit(solution)/shard_map/pallas_call | solution.py:349
  14.3 0.0 collective-permute-done.refs_1_
  14.3 0.0 collective-permute-done.6.refs_7_
  14.3 0.0 collective-permute-done.4.refs_5_
  14.3 0.0 collective-permute-done.2.refs_3_
  14.3 0.0 copy-start
  14.3 8.8 %shard_map.190 = (f32[1152,128]{1,0:T(8,128)S(1)}, f32[8,128]{1,0:T(8,128)S(1)}, bf16[128,768]{1,0:T(8,128)(2,1)S(1)}, bf16[128,768]{1,0:T(8,128)(2,1)S(1)}) custom-call(s32[2]{0:T(128)S(1)} %pad_add_fusion.place_ref, bf16[32,896]{1,0:T(8,128)(2,1)S(1)} %shard_map.188.refs_0_, bf16[32,896]{1,0:T(8,128)(2,1)S(1)} %collective-permute-done.refs_1_, ...), custom_call_target="tpu_custom_call" | custom-call | flops 6442450944 | bytes 3218432 | tf_op jit(solution)/shard_map/pallas_call | solution.py:349
  23.2 0.0 copy-start.1
  23.2 0.0 copy-start.5
  23.2 0.0 copy-start.6
  23.2 0.0 copy-start.7
  23.2 0.1 collective-permute-start.7
  23.3 2.0 %collective-permute-done.7.refs_1_ = f32[1152,128]{1,0:T(8,128)S(1)} collective-permute-done((f32[1152,128]{1,0:T(8,128)S(1)}, f32[1152,128]{1,0:T(8,128)S(1)}, u32[]{:S(2)}, u32[]{:S(2)}) %collective-permute-start.7) | collective-permute-done | bytes 589856 | tf_op jit(solution)/shard_map/ppermute | solution.py:318
  25.3 1.4 %shard_map.191 = (f32[80,768]{1,0:T(8,128)S(1)}, bf16[80,768]{1,0:T(8,128)(2,1)S(1)}, bf16[80,768]{1,0:T(8,128)(2,1)S(1)}, bf16[80,768]{1,0:T(8,128)(2,1)S(1)}, ...) custom-call(s32[2]{0:T(128)S(1)} %pad_add_fusion.place_ref, ...), custom_call_target="tpu_custom_call" | custom-call | flops 169869312 | bytes 3371008 | tf_op jit(solution)/shard_map/pallas_call | solution.py:349
  26.7 1.6 %collective-permute-start.8 = (bf16[80,768]{1,0:T(8,128)(2,1)S(1)}, bf16[80,768]{1,0:T(8,128)(2,1)S(1)}, u32[]{:S(2)}, u32[]{:S(2)}) collective-permute-start(bf16[80,768]{1,0:T(8,128)(2,1)S(1)} %get-tuple-element.43), channel_id=1, source_target_pairs={{0,8},{8,0},{16,24},{24,16},{1,9},{9,1},{17,25},{25,17},{2,10},{10... | collective-permute-start | bytes 368648 | tf_op jit(solution)/shard_map/ppermute | solution.py:318
  28.3 1.5 %collective-permute-start.9 = (bf16[80,768]{1,0:T(8,128)(2,1)S(1)}, bf16[80,768]{1,0:T(8,128)(2,1)S(1)}, u32[]{:S(2)}, u32[]{:S(2)}) collective-permute-start(bf16[80,768]{1,0:T(8,128)(2,1)S(1)} %get-tuple-element.44), channel_id=1, source_target_pairs={{0,16},{8,24},{16,0},{24,8},{1,17},{9,25},{17,1},{25,9},{2,18},{10... | collective-permute-start | bytes 368648 | tf_op jit(solution)/shard_map/ppermute | solution.py:318
  29.8 0.5 %collective-permute-start.10 = (bf16[80,768]{1,0:T(8,128)(2,1)S(1)}, bf16[80,768]{1,0:T(8,128)(2,1)S(1)}, u32[]{:S(2)}, u32[]{:S(2)}) collective-permute-start(bf16[80,768]{1,0:T(8,128)(2,1)S(1)} %get-tuple-element.45), channel_id=1, source_target_pairs={{0,24},{8,16},{16,8},{24,0},{1,25},{9,17},{17,9},{25,1},{2,26},{10... | collective-permute-start | bytes 368648 | tf_op jit(solution)/shard_map/ppermute | solution.py:318
  30.3 0.0 copy-done
  30.3 0.0 copy-done.1
  30.3 0.0 copy-done.5
  30.3 0.0 copy-done.6
  30.3 0.0 copy-done.7
  30.3 0.0 copy-start.2
  30.3 0.0 copy-start.3
  30.3 0.0 copy-start.4
  30.3 0.0 copy-start.8
  30.4 0.0 copy-start.9
  30.4 2.2 %shard_map.192 = (bf16[16,768]{1,0:T(8,128)(2,1)}, f32[16,768]{1,0:T(8,128)}) custom-call(s32[2]{0:T(128)S(1)} %pad_add_fusion.place_ref, f32[768,128]{1,0:T(8,128)S(1)} %get-tuple-element.37.active_ref, f32[768,128]{1,0:T(8,128)S(1)} %get-tuple-element.38.src_ref, f32[768,128]{1,0:T(8,128)S(1)} %get-tuple-element.39.dst_ref, ...), custom_call_target="tpu_custom_call" | custom-call | flops 452984832 | bytes 4851712 | tf_op jit(solution)/shard_map/pallas_call | solution.py:349
  32.6 0.0 collective-permute-done.8.refs_1_
  32.6 3.4 %collective-permute-done.9.refs_2_ = bf16[80,768]{1,0:T(8,128)(2,1)S(1)} collective-permute-done((bf16[80,768]{1,0:T(8,128)(2,1)S(1)}, bf16[80,768]{1,0:T(8,128)(2,1)S(1)}, u32[]{:S(2)}, u32[]{:S(2)}) %collective-permute-start.9) | collective-permute-done | bytes 122912 | tf_op jit(solution)/shard_map/ppermute | solution.py:318
  36.0 0.0 collective-permute-done.10.refs_3_
  36.0 0.0 copy-done.2
  36.0 0.0 copy-done.3
  36.0 0.0 copy-done.4
  36.0 0.0 copy-done.8
  36.0 1.1 %shard_map.193 = (f32[432,128]{1,0:T(8,128)}, f32[432,128]{1,0:T(8,128)}, f32[432,128]{1,0:T(8,128)}, f32[2,768]{1,0:T(2,128)}, f32[2,768]{1,0:T(2,128)}, /*index=5*/f32[2,768]{1,0:T(2,128)}) custom-call(f32[80,768]{1,0:T(8,128)S(1)} %get-tuple-element.42.refs_0_, bf16[80,768]{1,0:T(8,128)(2,1)S(1)} %collective-permute-done.8.refs_1_, ...), custom_call_target="tpu_custom_call" | custom-call | bytes 1978368 | tf_op jit(solution)/shard_map/pallas_call | solution.py:349
  (1 shorter events, 0.0 us)
Async XLA Ops:
  1.5 7.5 %collective-permute-start.5 = (bf16[32,896]{1,0:T(8,128)(2,1)S(1)}, bf16[32,896]{1,0:T(8,128)(2,1)S(1)}, u32[]{:S(2)}, u32[]{:S(2)}) collective-permute-start(bf16[32,896]{1,0:T(8,128)(2,1)S(1)} %shard_map.188.refs_0_), channel_id=1, source_target_pairs={{0,6},{1,7},{2,4},{3,5},{4,2},{5,3},{6,0},{7,1},{8,14},{9,15},{10,... | collective-permute-start | bytes 172040 | tf_op jit(solution)/shard_map/ppermute | solution.py:318
  6.6 5.1 %collective-permute-start.3 = (bf16[32,896]{1,0:T(8,128)(2,1)S(1)}, bf16[32,896]{1,0:T(8,128)(2,1)S(1)}, u32[]{:S(2)}, u32[]{:S(2)}) collective-permute-start(bf16[32,896]{1,0:T(8,128)(2,1)S(1)} %shard_map.188.refs_0_), channel_id=1, source_target_pairs={{0,4},{1,5},{2,6},{3,7},{4,0},{5,1},{6,2},{7,3},{8,12},{9,13},{10,... | collective-permute-start | bytes 172040 | tf_op jit(solution)/shard_map/ppermute | solution.py:318
  6.6 5.1 %collective-permute-start.1 = (bf16[32,896]{1,0:T(8,128)(2,1)S(1)}, bf16[32,896]{1,0:T(8,128)(2,1)S(1)}, u32[]{:S(2)}, u32[]{:S(2)}) collective-permute-start(bf16[32,896]{1,0:T(8,128)(2,1)S(1)} %shard_map.188.refs_0_), channel_id=1, source_target_pairs={{0,2},{1,3},{2,0},{3,1},{4,6},{5,7},{6,4},{7,5},{8,10},{9,11},{10,... | collective-permute-start | bytes 172040 | tf_op jit(solution)/shard_map/ppermute | solution.py:318
  7.3 7.0 %collective-permute-start = (bf16[32,896]{1,0:T(8,128)(2,1)S(1)}, bf16[32,896]{1,0:T(8,128)(2,1)S(1)}, u32[]{:S(2)}, u32[]{:S(2)}) collective-permute-start(bf16[32,896]{1,0:T(8,128)(2,1)S(1)} %shard_map.188.refs_0_), channel_id=1, source_target_pairs={{0,1},{1,0},{2,3},{3,2},{4,5},{5,4},{6,7},{7,6},{8,9},{9,8},{10,11... | collective-permute-start | bytes 172040 | tf_op jit(solution)/shard_map/ppermute | solution.py:318
  8.9 5.4 %collective-permute-start.6 = (bf16[32,896]{1,0:T(8,128)(2,1)S(1)}, bf16[32,896]{1,0:T(8,128)(2,1)S(1)}, u32[]{:S(2)}, u32[]{:S(2)}) collective-permute-start(bf16[32,896]{1,0:T(8,128)(2,1)S(1)} %collective-permute-done.5.refs_6_), channel_id=1, source_target_pairs={{0,1},{1,0},{2,3},{3,2},{4,5},{5,4},{6,7},{7,6},{8,9},{9,8},{10,11... | collective-permute-start | bytes 172040 | tf_op jit(solution)/shard_map/ppermute | solution.py:318
  11.7 2.6 %collective-permute-start.4 = (bf16[32,896]{1,0:T(8,128)(2,1)S(1)}, bf16[32,896]{1,0:T(8,128)(2,1)S(1)}, u32[]{:S(2)}, u32[]{:S(2)}) collective-permute-start(bf16[32,896]{1,0:T(8,128)(2,1)S(1)} %collective-permute-done.3.refs_4_), channel_id=1, source_target_pairs={{0,1},{1,0},{2,3},{3,2},{4,5},{5,4},{6,7},{7,6},{8,9},{9,8},{10,11... | collective-permute-start | bytes 172040 | tf_op jit(solution)/shard_map/ppermute | solution.py:318
  11.7 2.6 %collective-permute-start.2 = (bf16[32,896]{1,0:T(8,128)(2,1)S(1)}, bf16[32,896]{1,0:T(8,128)(2,1)S(1)}, u32[]{:S(2)}, u32[]{:S(2)}) collective-permute-start(bf16[32,896]{1,0:T(8,128)(2,1)S(1)} %collective-permute-done.1.refs_2_), channel_id=1, source_target_pairs={{0,1},{1,0},{2,3},{3,2},{4,5},{5,4},{6,7},{7,6},{8,9},{9,8},{10,11... | collective-permute-start | bytes 172040 | tf_op jit(solution)/shard_map/ppermute | solution.py:318
  14.3 16.0 %copy-start = (bf16[1536,768]{1,0:T(8,128)(2,1)S(1)}, bf16[1536,768]{1,0:T(8,128)(2,1)}, u32[]{:S(2)}) copy-start(bf16[1536,768]{1,0:T(8,128)(2,1)} %first_ref.3) | copy-start | bytes 7077892
  23.2 7.1 %copy-start.1 = (bf16[768,768]{1,0:T(8,128)(2,1)S(1)}, bf16[768,768]{1,0:T(8,128)(2,1)}, u32[]{:S(2)}) copy-start(bf16[768,768]{1,0:T(8,128)(2,1)} %second_ref.3) | copy-start | bytes 3538948
  23.2 7.1 %copy-start.5 = (bf16[1,16,768]{2,1,0:T(8,128)(2,1)S(1)}, bf16[1,16,768]{2,1,0:T(8,128)(2,1)}, u32[]{:S(2)}) copy-start(bf16[1,16,768]{2,1,0:T(8,128)(2,1)} %param.13) | copy-start | bytes 73732
  23.2 7.1 %copy-start.6 = (bf16[1,16,768]{2,1,0:T(8,128)(2,1)S(1)}, bf16[1,16,768]{2,1,0:T(8,128)(2,1)}, u32[]{:S(2)}) copy-start(bf16[1,16,768]{2,1,0:T(8,128)(2,1)} %param.14) | copy-start | bytes 73732
  23.2 7.1 %copy-start.7 = (f32[2,768]{1,0:T(2,128)S(1)}, f32[2,768]{1,0:T(2,128)}, u32[]{:S(2)}) copy-start(f32[2,768]{1,0:T(2,128)} %refs_7_.1) | copy-start | bytes 18436
  23.2 2.1 %collective-permute-start.7 = (f32[1152,128]{1,0:T(8,128)S(1)}, f32[1152,128]{1,0:T(8,128)S(1)}, u32[]{:S(2)}, u32[]{:S(2)}) collective-permute-start(f32[1152,128]{1,0:T(8,128)S(1)} %get-tuple-element.33.refs_0_), channel_id=1, source_target_pairs={{0,1},{1,0},{2,3},{3,2},{4,5},{5,4},{6,7},{7,6},{8,9},{9,8},{10,11... | collective-permute-start | bytes 1769480 | tf_op jit(solution)/shard_map/ppermute | solution.py:318
  26.7 5.9 %collective-permute-start.8 = (bf16[80,768]{1,0:T(8,128)(2,1)S(1)}, bf16[80,768]{1,0:T(8,128)(2,1)S(1)}, u32[]{:S(2)}, u32[]{:S(2)}) collective-permute-start(bf16[80,768]{1,0:T(8,128)(2,1)S(1)} %get-tuple-element.43), channel_id=1, source_target_pairs={{0,8},{8,0},{16,24},{24,16},{1,9},{9,1},{17,25},{25,17},{2,10},{10... | collective-permute-start | bytes 368648 | tf_op jit(solution)/shard_map/ppermute | solution.py:318
  28.3 7.7 %collective-permute-start.9 = (bf16[80,768]{1,0:T(8,128)(2,1)S(1)}, bf16[80,768]{1,0:T(8,128)(2,1)S(1)}, u32[]{:S(2)}, u32[]{:S(2)}) collective-permute-start(bf16[80,768]{1,0:T(8,128)(2,1)S(1)} %get-tuple-element.44), channel_id=1, source_target_pairs={{0,16},{8,24},{16,0},{24,8},{1,17},{9,25},{17,1},{25,9},{2,18},{10... | collective-permute-start | bytes 368648 | tf_op jit(solution)/shard_map/ppermute | solution.py:318
  29.8 6.2 %collective-permute-start.10 = (bf16[80,768]{1,0:T(8,128)(2,1)S(1)}, bf16[80,768]{1,0:T(8,128)(2,1)S(1)}, u32[]{:S(2)}, u32[]{:S(2)}) collective-permute-start(bf16[80,768]{1,0:T(8,128)(2,1)S(1)} %get-tuple-element.45), channel_id=1, source_target_pairs={{0,24},{8,16},{16,8},{24,0},{1,25},{9,17},{17,9},{25,1},{2,26},{10... | collective-permute-start | bytes 368648 | tf_op jit(solution)/shard_map/ppermute | solution.py:318
  30.3 5.7 %copy-start.2 = (f32[55296]{0:T(1024)S(1)}, f32[55296]{0:T(1024)}, u32[]{:S(2)}) copy-start(f32[55296]{0:T(1024)} %param.21) | copy-start | bytes 663556
  30.3 5.7 %copy-start.3 = (f32[55296]{0:T(1024)S(1)}, f32[55296]{0:T(1024)}, u32[]{:S(2)}) copy-start(f32[55296]{0:T(1024)} %param.22) | copy-start | bytes 663556
  30.3 5.7 %copy-start.4 = (f32[55296]{0:T(1024)S(1)}, f32[55296]{0:T(1024)}, u32[]{:S(2)}) copy-start(f32[55296]{0:T(1024)} %param.23) | copy-start | bytes 663556
  30.3 5.7 %copy-start.8 = (f32[2,768]{1,0:T(2,128)S(1)}, f32[2,768]{1,0:T(2,128)}, u32[]{:S(2)}) copy-start(f32[2,768]{1,0:T(2,128)} %refs_8_.1) | copy-start | bytes 18436
  30.4 5.7 %copy-start.9 = (f32[2,768]{1,0:T(2,128)S(1)}, f32[2,768]{1,0:T(2,128)}, u32[]{:S(2)}) copy-start(f32[2,768]{1,0:T(2,128)} %refs_9_.1) | copy-start | bytes 18436
